TPU v7x, 32 devices: a whole 2x2x4 slice. The times are simulated.
32 devices in a mesh: groups: 2 (over y), expert: 8 (over z, core), section: 2 (over x), tensor: 1.
Axes of the slice: x: 2, y: 2, z: 4, core: 2. Of those that a mesh axis runs over, the one named last changes fastest.
Arguments:
- opening_residual: bfloat16 [2, 2048, 2048], P('section', ('groups', 'expert'), 'tensor'), parts along dimension 1, may hold values from -12 to 12
- incoming_residual: bfloat16 [1, 2048, 2048], P(None, ('groups', 'expert'), 'tensor'), parts along dimension 1, may hold values from -12 to 12
- stored_summaries: bfloat16 [2, 2, 16, 768, 512], P(None, 'section', ('groups', 'expert')), parts along dimension 2, may hold values from -40 to 40
- stored_counts: int32 [3, 16], P(None, ('groups', 'expert')), parts along dimension 1, may hold values from 1 to 768, as said below
- picked_specialists: int32 [2, 2, 2048, 6], P(None, 'section', ('groups', 'expert')), parts along dimension 2, may hold values from 0 to 15, all different within a row; in each aligned block of 128 rows (0 to 127, 128 to 255, ..., all dimensions but the last counted through in order) at most 64 rows name the same one
- chooser_mixing_share: float32 [2, 2, 2048, 6], P(None, 'section', ('groups', 'expert')), parts along dimension 2, may hold values from 0.05 to 0.4
- mixing_scale_factor: float32 [2, 2048], P('section'), may hold values from 0.25 to 1.75
- asking_projection: bfloat16 [2, 2048, 1024], P('section', None, 'tensor'), may hold values from -0.125 to 0.125
- summary_lookup_factor: bfloat16 [2, 8, 128, 512], P('section', 'tensor'), may hold values from -0.5 to 0.5
- summary_content_factor: bfloat16 [2, 8, 512, 128], P('section', 'tensor'), may hold values from -0.25 to 0.25
- merging_projection: bfloat16 [2, 1024, 2048], P('section', 'tensor'), may hold values from -0.1875 to 0.1875
- compress_projection: bfloat16 [2, 2048, 512], P('section', None, 'tensor'), may hold values from -0.125 to 0.125
- summary_scale_factor: float32 [2, 512], P('section'), may hold values from 0.25 to 1.75
- specialist_scale_factor: float32 [2, 2048], P('section', 'tensor'), may hold values from 0.25 to 1.75
- specialist_switch_factor: bfloat16 [2, 16, 2048, 704], P('section', 'expert', None, 'tensor'), may hold values from -0.125 to 0.125
- specialist_widen_factor: bfloat16 [2, 16, 2048, 704], P('section', 'expert', None, 'tensor'), may hold values from -0.125 to 0.125
- specialist_contract_factor: bfloat16 [2, 16, 704, 2048], P('section', 'expert', 'tensor'), may hold values from -0.21875 to 0.21875
Outputs:
- results: bfloat16 [2, 2, 2048, 2048], P(None, 'section', ('groups', 'expert'), 'tensor'), parts along dimension 2
There are 2 independent parts, one for each index of `groups`. A program takes and returns all parts, laid end to end along the dimension named above; an argument that names none is the same for every part. Nothing has to cross between parts.
Inputs may be any that keep to these rules, and one draw needn't show every extreme that they name: `picked_specialists`: in each aligned block of 128 rows (one sequence) no expert is chosen by more than 64 rows, a bound that some block reaches; each row names 6 different experts. `stored_counts`: in every microbatch some sequence has exactly 768 cached tokens.
All inputs are finite; a program needn't handle non-finite values.
Results may differ from a plain program's by a relative error of at most 0.04.
Values may be sent and summed in bfloat16 or wider, within the bound.
A program may use at most 128 MiB of HBM per device.

v0:
```python
import jax
import jax.numpy as jnp
from jax import lax
from jax.experimental import pallas as pl
from jax.experimental.pallas import tpu as pltpu
from jax.sharding import PartitionSpec as P

CAP = 64
RETURN_CHUNKS = 2


epsilon = 1e-06


MESH = pl.DeviceIdType.MESH
PIECES = 2


def place_on_line():
    count = lax.axis_size("expert")
    pair = 2 if count % 2 == 0 else 1
    mine = lax.axis_index("expert")
    return count // pair, pair, mine, mine // pair, lax.rem(mine, pair)


def greet(chips, pair, mine, spot, side):
    barrier = pltpu.get_barrier_semaphore()

    def hello(other):
        pl.semaphore_signal(barrier, inc=1, device_id={"expert": other}, device_id_type=MESH)

    @pl.when(spot > 0)
    def _():
        hello(mine - pair)

    @pl.when(spot < chips - 1)
    def _():
        hello(mine + pair)

    if pair == 2:
        hello(mine + 1 - 2 * side)
    inner = (spot > 0) & (spot < chips - 1)

    @pl.when(inner)
    def _():
        pl.semaphore_wait(barrier, pair + 1)

    @pl.when(jnp.logical_not(inner))
    def _():
        pl.semaphore_wait(barrier, pair)


def remote(src, dst, send, recv, other):
    return pltpu.make_async_remote_copy(
        src_ref=src,
        dst_ref=dst,
        send_sem=send,
        recv_sem=recv,
        device_id={"expert": other},
        device_id_type=MESH,
    )


def spread_kernel(
    own_ref, small_ref, all_ref, small_all_ref, own_sem, line_send, line_recv, side_send, side_recv
):
    chips, pair, mine, spot, side = place_on_line()
    step = own_ref.shape[0] // PIECES
    sibling = mine + 1 - 2 * side

    def rows(block, core, piece):
        if piece == PIECES:
            return small_all_ref.at[block, core]
        return all_ref.at[block, core, pl.ds(piece * step, step)]

    def origin(block, piece):
        if block is not None:
            return rows(block, side, piece)
        return small_ref if piece == PIECES else own_ref.at[pl.ds(piece * step, step)]

    def line_copy(block, piece, way):
        source = origin(block, piece)
        where = spot if block is None else block
        direction = 0 if way > 0 else 1
        return remote(
            source,
            rows(where, side, piece),
            line_send.at[direction, where, piece],
            line_recv.at[where, piece],
            mine + way * pair,
        )

    def side_copy(block, piece):
        source = origin(block, piece)
        where = spot if block is None else block
        return remote(
            source,
            rows(where, side, piece),
            side_send.at[where, piece],
            side_recv.at[where, piece],
            sibling,
        )

    def onward(block, piece, way, act):
        @pl.when((spot < chips - 1) if way > 0 else (spot > 0))
        def _():
            act(line_copy(block, piece, way))

    greet(chips, pair, mine, spot, side)
    for piece in range(PIECES + 1):
        for way in (1, -1):
            onward(None, piece, way, lambda copy: copy.start())
    for piece in range(PIECES + 1):
        if pair == 2:
            side_copy(None, piece).start()
    keep = pltpu.make_async_copy(own_ref, all_ref.at[spot, side], own_sem.at[0])
    keep.start()
    keep_small = pltpu.make_async_copy(small_ref, small_all_ref.at[spot, side], own_sem.at[1])
    keep_small.start()
    for far in range(1, chips):
        for piece in range(PIECES + 1):
            for way in (1, -1):
                block = spot - way * far

                @pl.when((block >= 0) if way > 0 else (block < chips))
                def _():
                    line_copy(block, piece, way).wait_recv()
                    onward(block, piece, way, lambda copy: copy.start())
                    if pair == 2:
                        side_copy(block, piece).start()

    keep.wait()
    keep_small.wait()
    for piece in range(PIECES + 1):
        for way in (1, -1):
            onward(None, piece, way, lambda copy: copy.wait_send())
        if pair == 2:
            side_copy(None, piece).wait()
    for far in range(1, chips):
        for piece in range(PIECES + 1):
            for way in (1, -1):
                block = spot - way * far

                @pl.when((block >= 0) if way > 0 else (block < chips))
                def _():
                    onward(block, piece, way, lambda copy: copy.wait_send())
                    if pair == 2:
                        side_copy(block, piece).wait()


def spread(own, small):
    count = lax.axis_size("expert")
    pair = 2 if count % 2 == 0 else 1
    chips = count // pair
    held = count * own.size * own.dtype.itemsize
    result, small_result = pl.pallas_call(
        spread_kernel,
        out_shape=[
            jax.ShapeDtypeStruct((chips, pair) + own.shape, own.dtype),
            jax.ShapeDtypeStruct((chips, pair) + small.shape, small.dtype),
        ],
        in_specs=[pl.BlockSpec(memory_space=pltpu.VMEM)] * 2,
        out_specs=[pl.BlockSpec(memory_space=pltpu.VMEM)] * 2,
        scratch_shapes=[
            pltpu.SemaphoreType.DMA((2,)),
            pltpu.SemaphoreType.DMA((2, chips, PIECES + 1)),
            pltpu.SemaphoreType.DMA((chips, PIECES + 1)),
            pltpu.SemaphoreType.DMA((chips, PIECES + 1)),
            pltpu.SemaphoreType.DMA((chips, PIECES + 1)),
        ],
        compiler_params=pltpu.CompilerParams(
            collective_id=0, has_side_effects=True, vmem_limit_bytes=2 * held
        ),
        cost_estimate=pl.CostEstimate(flops=0, bytes_accessed=32 * held, transcendentals=0),
    )(own, small)
    return result.reshape((count,) + own.shape), small_result.reshape((count,) + small.shape)


def gather_sum_kernel(*refs):
    part_refs, refs = refs[:RETURN_CHUNKS], refs[RETURN_CHUNKS:]
    sum_ref, side_in, total, line_in, side_send, side_recv, line_send, line_recv = refs
    chips, pair, mine, spot, side = place_on_line()
    chunk = part_refs[0].shape[3]
    sibling = mine + 1 - 2 * side

    def side_copy(block, piece):
        return remote(
            part_refs[piece].at[block, 1 - side],
            side_in.at[block, piece],
            side_send.at[block, piece],
            side_recv.at[block, piece],
            sibling,
        )

    def line_copy(block, piece, way):
        direction = 0 if way > 0 else 1
        return remote(
            total.at[block, piece],
            line_in.at[direction, block, piece],
            line_send.at[block, piece],
            line_recv.at[direction, block, piece],
            mine + way * pair,
        )

    def wide(value):
        return value.astype(jnp.float32)

    def chip_sum(block, piece):
        value = wide(part_refs[piece][block, side])
        if pair == 2:
            side_copy(block, piece).wait_recv()
            value = value + wide(side_in[block, piece])
        return value

    greet(chips, pair, mine, spot, side)
    if pair == 2:
        for far in range(chips - 1, -1, -1):
            for piece in range(RETURN_CHUNKS):
                for way in (1, -1) if far else (1,):
                    block = spot + way * far

                    @pl.when((block >= 0) & (block < chips))
                    def _():
                        side_copy(block, piece).start()

    for far in range(chips - 1, 0, -1):
        for piece in range(RETURN_CHUNKS):
            for way in (1, -1):
                block = spot + way * far

                @pl.when((block >= 0) & (block < chips))
                def _():
                    value = chip_sum(block, piece)
                    total[block, piece] = value.astype(total.dtype)
                    if far < chips - 1:

                        @pl.when((spot > 0) if way > 0 else (spot < chips - 1))
                        def _():
                            direction = 0 if way > 0 else 1
                            line_copy(block, piece, way).wait_recv()
                            total[block, piece] = (
                                wide(total[block, piece])
                                + wide(line_in[direction, block, piece])
                            ).astype(total.dtype)

                    line_copy(block, piece, way).start()

    for piece in range(RETURN_CHUNKS):
        total[spot, piece] = chip_sum(spot, piece).astype(total.dtype)
        for way in (1, -1):

            @pl.when((spot > 0) if way > 0 else (spot < chips - 1))
            def _():
                direction = 0 if way > 0 else 1
                line_copy(spot, piece, way).wait_recv()
                total[spot, piece] = (
                    wide(total[spot, piece]) + wide(line_in[direction, spot, piece])
                ).astype(total.dtype)

        sum_ref[:, pl.ds(piece * chunk, chunk)] = total[spot, piece]
    for far in range(chips - 1, -1, -1):
        for piece in range(RETURN_CHUNKS):
            for way in (1, -1) if far else (1,):
                block = spot + way * far

                @pl.when((block >= 0) & (block < chips))
                def _():
                    if far:
                        line_copy(block, piece, way).wait_send()
                    if pair == 2:
                        side_copy(block, piece).wait_send()


def gather_sum(parts):
    count, height, chunk = parts[0].shape
    pieces = len(parts)
    kind = parts[0].dtype
    held = pieces * parts[0].size * kind.itemsize
    pair = 2 if count % 2 == 0 else 1
    chips = count // pair
    return pl.pallas_call(
        gather_sum_kernel,
        out_shape=jax.ShapeDtypeStruct((height, pieces * chunk), kind),
        in_specs=[pl.BlockSpec(memory_space=pltpu.VMEM)] * pieces,
        out_specs=pl.BlockSpec(memory_space=pltpu.VMEM),
        scratch_shapes=[
            pltpu.VMEM((chips, pieces, height, chunk), kind),
            pltpu.VMEM((chips, pieces, height, chunk), kind),
            pltpu.VMEM((2, chips, pieces, height, chunk), kind),
            pltpu.SemaphoreType.DMA((chips, pieces)),
            pltpu.SemaphoreType.DMA((chips, pieces)),
            pltpu.SemaphoreType.DMA((chips, pieces)),
            pltpu.SemaphoreType.DMA((2, chips, pieces)),
        ],
        compiler_params=pltpu.CompilerParams(
            collective_id=1, has_side_effects=True, vmem_limit_bytes=4 * held
        ),
        cost_estimate=pl.CostEstimate(flops=0, bytes_accessed=32 * held, transcendentals=0),
    )(*[part.reshape(chips, pair, height, chunk) for part in parts])


def shifted(value, axis, steps):
    count = lax.axis_size(axis)
    initial, last = (max(0, -steps), min(count, count - steps))
    return lax.ppermute(value, axis, [(source, source + steps) for source in range(initial, last)])


def row_norm(values, gain_row):
    return (
        values * lax.rsqrt(jnp.mean(values * values, axis=-1, keepdims=True) + epsilon) * gain_row
    )


def attend(q_lat, cache_rows, new_rows, length, score_scale):
    piece_list = q_lat.shape[0]
    context = cache_rows.shape[0]
    key_rows = jnp.concatenate([cache_rows, new_rows], axis=0)
    scores = (
        jnp.einsum("thl,kl->thk", q_lat, key_rows, preferred_element_type=jnp.float32) * score_scale
    )
    position = lax.broadcasted_iota(jnp.int32, (piece_list, context + piece_list), 1)
    query_pos = lax.broadcasted_iota(jnp.int32, (piece_list, context + piece_list), 0)
    visible = jnp.where(position < context, position < length, position - context <= query_pos)
    scores = jnp.where(visible[:, None, :], scores, -jnp.inf)
    row_max = jnp.max(scores, axis=-1, keepdims=True)
    expd = jnp.where(visible[:, None, :], jnp.exp(scores - row_max), 0.0)
    attention = (expd / jnp.sum(expd, axis=-1, keepdims=True)).astype(jnp.bfloat16)
    return jnp.einsum(
        "thk,kl->thl", attention, key_rows, preferred_element_type=jnp.float32
    ).astype(jnp.bfloat16)


def shards(
    opening_residual,
    incoming_residual,
    stored_summaries,
    stored_counts,
    picked_specialists,
    chooser_mixing_share,
    mixing_scale_factor,
    asking_projection,
    summary_lookup_factor,
    summary_content_factor,
    merging_projection,
    compress_projection,
    summary_scale_factor,
    specialist_scale_factor,
    specialist_switch_factor,
    specialist_widen_factor,
    specialist_contract_factor,
):
    segment_ordinal = lax.axis_index("section")
    section_count = lax.axis_size("section")
    sources = lax.axis_size("expert")
    tick_count = stored_summaries.shape[0]
    piece_list = opening_residual.shape[1]
    inner_feature_midcount = opening_residual.shape[2]
    full_width = mixing_scale_factor.shape[1]
    local_heads = summary_lookup_factor.shape[1]
    head_size = summary_lookup_factor.shape[2]
    top_count = picked_specialists.shape[3]
    expert_local = specialist_switch_factor.shape[1]
    score_scale = head_size ** (-0.5)
    expert_ids = lax.broadcasted_iota(jnp.int32, (1, 1, 1, expert_local * sources), 3)
    shares_dense = jnp.sum(
        jnp.where(
            picked_specialists[:, 0][..., None] == expert_ids,
            chooser_mixing_share[:, 0][..., None],
            0.0,
        ),
        axis=2,
    )
    shares_dense = jnp.swapaxes(shares_dense, 1, 2)
    earlier_or_same = (
        lax.broadcasted_iota(jnp.int32, (piece_list, piece_list), 0)
        <= lax.broadcasted_iota(jnp.int32, (piece_list, piece_list), 1)
    ).astype(jnp.bfloat16)
    slots = lax.broadcasted_iota(jnp.int32, (1, 1, CAP, 1), 2) + 1
    outputs = []
    present_carry = opening_residual[0]
    section_out = present_carry
    for step_index in range(tick_count):
        if step_index > 0:
            handed = shifted(section_out, "section", 1)
            present_carry = jnp.where(
                segment_ordinal == 0, incoming_residual[step_index - 1], handed
            )
        micro_index = step_index - segment_ordinal + section_count - 1
        length = lax.dynamic_index_in_dim(stored_counts[:, 0], micro_index, 0, keepdims=False)
        full_rows = lax.all_gather(present_carry, "tensor", axis=1, tiled=True)
        normed = row_norm(full_rows.astype(jnp.float32), mixing_scale_factor[0]).astype(
            jnp.bfloat16
        )
        queries = jnp.dot(normed, asking_projection[0], preferred_element_type=jnp.float32).astype(
            jnp.bfloat16
        )
        queries = queries.reshape(piece_list, local_heads, head_size)
        q_lat = jnp.einsum(
            "thd,hdl->thl", queries, summary_lookup_factor[0], preferred_element_type=jnp.float32
        ).astype(jnp.bfloat16)
        latent_part = jnp.dot(normed, compress_projection[0], preferred_element_type=jnp.float32)
        latent_raw = lax.all_gather(
            latent_part.astype(jnp.bfloat16), "tensor", axis=1, tiled=True
        ).astype(latent_part.dtype)
        new_latent = row_norm(latent_raw, summary_scale_factor[0]).astype(jnp.bfloat16)
        o_lat = attend(q_lat, stored_summaries[step_index, 0, 0], new_latent, length, score_scale)
        heads_out = jnp.einsum(
            "thl,hld->thd", o_lat, summary_content_factor[0], preferred_element_type=jnp.float32
        ).astype(jnp.bfloat16)
        heads_out = heads_out.reshape(piece_list, local_heads * head_size)
        head_terms = jnp.dot(heads_out, merging_projection[0], preferred_element_type=jnp.float32)
        residual = present_carry.astype(jnp.float32) + lax.psum_scatter(
            head_terms.astype(jnp.bfloat16), "tensor", scatter_dimension=1, tiled=True
        ).astype(jnp.float32)
        squares = lax.psum(jnp.sum(residual * residual, axis=1), "tensor")
        moe_input = (
            residual
            * lax.rsqrt(squares / full_width + epsilon)[:, None]
            * specialist_scale_factor[0]
        ).astype(jnp.bfloat16)
        whole_rows = lax.all_gather(moe_input, "tensor", axis=1, tiled=True)
        all_rows, all_shares = spread(whole_rows, shares_dense[step_index])
        mine = lax.dynamic_slice_in_dim(
            all_shares, lax.axis_index("expert") * expert_local, expert_local, axis=1
        )
        chosen = mine > 0.0
        rank = jnp.einsum(
            "jer,rq->jeq",
            chosen.astype(jnp.bfloat16),
            earlier_or_same,
            preferred_element_type=jnp.float32,
        ).astype(jnp.int32)
        at_slot = (rank[..., None, :] == slots) & chosen[..., None, :]
        place = at_slot.astype(jnp.bfloat16)
        share = jnp.sum(jnp.where(at_slot, mine[..., None, :], 0.0), axis=-1)
        hidden_list = []
        for e in range(expert_local):
            rows_in = jnp.einsum(
                "jsr,jrd->jsd", place[:, e], all_rows, preferred_element_type=jnp.float32
            ).astype(jnp.bfloat16)
            rows_in = rows_in.reshape(sources * CAP, full_width)
            gate_values = jnp.dot(
                rows_in, specialist_switch_factor[0, e], preferred_element_type=jnp.float32
            )
            up_values = jnp.dot(
                rows_in, specialist_widen_factor[0, e], preferred_element_type=jnp.float32
            )
            hidden_list.append(
                (jax.nn.silu(gate_values) * up_values * share[:, e].reshape(-1, 1)).astype(
                    jnp.bfloat16
                )
            )
        chunk = full_width // RETURN_CHUNKS
        routed_list = []
        for c in range(RETURN_CHUNKS):
            total = None
            for e in range(expert_local):
                down = jnp.dot(
                    hidden_list[e],
                    specialist_contract_factor[0, e][:, c * chunk : (c + 1) * chunk],
                    preferred_element_type=jnp.float32,
                ).astype(jnp.bfloat16)
                term = jnp.einsum(
                    "jsr,jsd->jrd",
                    place[:, e],
                    down.reshape(sources, CAP, chunk),
                    preferred_element_type=jnp.float32,
                )
                total = term if total is None else total + term
            routed_list.append(total.astype(jnp.bfloat16))
        routed = gather_sum(routed_list)
        routed = lax.psum_scatter(routed, "tensor", scatter_dimension=1, tiled=True).astype(
            jnp.float32
        )
        section_out = (residual + routed).astype(jnp.bfloat16)
        outputs.append(section_out)
    return jnp.stack(outputs)[:, None]


def solution(mesh):
    in_specs = (
        P("section", ("groups", "expert"), "tensor"),
        P(None, ("groups", "expert"), "tensor"),
        P(None, "section", ("groups", "expert"), None, None),
        P(None, ("groups", "expert")),
        P(None, "section", ("groups", "expert"), None),
        P(None, "section", ("groups", "expert"), None),
        P("section", None),
        P("section", None, "tensor"),
        P("section", "tensor", None, None),
        P("section", "tensor", None, None),
        P("section", "tensor", None),
        P("section", None, "tensor"),
        P("section", None),
        P("section", "tensor"),
        P("section", "expert", None, "tensor"),
        P("section", "expert", None, "tensor"),
        P("section", "expert", "tensor", None),
    )
    out_specs = P(None, "section", ("groups", "expert"), "tensor")
    return jax.shard_map(shards, mesh=mesh, in_specs=in_specs, out_specs=out_specs, check_vma=False)
```

profile of v0, /device:TPU:14, one launch (start us, length us, event | category | flops | bytes accessed | tf_op | source)
XLA Modules:
  0.0 297.2 jit_solution(6589346234186189298)
XLA Ops:
  4.4 3.2 %fusion.130 = bf16[16,8,8,128]{3,2,1,0:T(8,128)(2,1)S(1)} fusion(bf16[1,2048,1024]{2,1,0:T(8,128)(2,1)} %param.24, bf16[1,128,2048]{2,1,0:T(8,128)(2,1)} %param.17, f32[2048]{0:T(1024)} %bitcast.304, f32[128]{0:T(128)S(1)} %add_rsqrt_fusion.5), kind=kOutput, calls=%fused_computation.118 | convolution fusion | flops 538050560 | bytes 4989440 | tf_op jit(solution)/shard_map/dot_general | solution.py:394
  15.1 4.5 %fusion.105 = f32[128,8,896]{2,0,1:T(8,128)} fusion(bf16[1,8,128,512]{3,2,1,0:T(8,128)(2,1)S(1)} %copy-done.5, bf16[128,512]{1,0:T(8,128)(2,1)S(1)} %multiply_convert_fusion.3, bf16[768,512]{1,0:T(8,128)(2,1)} %get-tuple-element.18, bf16[16,8,8,128]{3,2,1,0:T(8,128)(2,1)S(1)} %fusion.130), kind=kOutput, calls=%fused_computation.97 | convolution fusion | flops 1076101120 | bytes 5898240 | tf_op jit(solution)/shard_map/thl,kl->thk/dot_general | solution.py:319
  19.6 6.8 %fusion.192 = (f32[128,8]{0,1:T(8,128)S(1)}, f32[128,8,896]{2,0,1:T(8,128)}) fusion(f32[128,8,896]{2,0,1:T(8,128)} %fusion.105, pred[128,896]{1,0:T(8,128)(4,1)} %get-tuple-element.26), kind=kOutput, calls=%fused_computation.207 | output fusion | flops 6423423 | bytes 7458816 | tf_op jit(solution)/shard_map/sub | solution.py:326
  26.4 3.9 %fusion.126 = bf16[8,128,128]{1,2,0:T(8,128)(2,1)S(1)} fusion(f32[128,8,896]{2,0,1:T(8,128)} %get-tuple-element.32, f32[128,8]{0,1:T(8,128)S(1)} %get-tuple-element.31, bf16[1,8,512,128]{3,2,1,0:T(8,128)(2,1)} %param.26, bf16[128,512]{1,0:T(8,128)(2,1)S(1)} %multiply_convert_fusion.3, bf16[768,512]{1,0:T(8,128)(2,1)S(1)} %copy-done.8), kind=kOutput, calls=%fused_computation.116 | convolution fusion | flops 1078067200 | bytes 5902336 | tf_op jit(solution)/shard_map/thl,hld->thd/dot_general | solution.py:407
  30.4 3.1 %multiply_reduce_fusion.1 = (f32[128]{0:T(128)S(1)}, f32[128,2048]{1,0:T(8,128)S(1)}) fusion(bf16[128,1024]{0,1:T(8,128)(2,1)S(1)} %bitcast.302, bf16[1,1024,2048]{2,1,0:T(8,128)(2,1)} %param.27, bf16[1,128,2048]{2,1,0:T(8,128)(2,1)} %param.17), kind=kOutput, calls=%fused_computation.141 | convolution fusion | flops 538443648 | bytes 6029824 | tf_op jit(solution)/shard_map/dot_general | solution.py:411
  33.7 36.4 %shard_map.163 = (bf16[4,2,128,2048]{3,2,1,0:T(8,128)(2,1)S(1)}, f32[4,2,16,128]{3,2,1,0:T(8,128)S(1)}) custom-call(bf16[128,2048]{1,0:T(8,128)(2,1)S(1)} %multiply_convert_fusion.1.own_ref, f32[16,128]{1,0:T(8,128)S(1)} %get-tuple-element.20.small_ref), custom_call_target="tpu_custom_call" | custom-call | bytes 134217728 | tf_op jit(solution)/shard_map/pallas_call | solution.py:156
  74.9 5.4 %slice_bitcast_fusion = (bf16[704,2048]{1,0:T(8,128)(2,1)S(1)}, bf16[704,2048]{1,0:T(8,128)(2,1)}) fusion(bf16[1,2,704,2048]{3,2,1,0:T(8,128)(2,1)} %param.33), kind=kLoop, calls=%fused_computation.40 | loop fusion | bytes 11534336 | tf_op jit(solution)/shard_map/squeeze | solution.py:460
  80.3 4.5 %fusion.16 = f32[512,704]{0,1:T(8,128)S(1)} fusion(bf16[512,2048]{1,0:T(8,128)(2,1)S(1)} %bitcast.289, bf16[1,2,2048,704]{2,3,1,0:T(8,128)(2,1)} %param.31), kind=kOutput, calls=%fused_computation.30 | convolution fusion | flops 1476395008 | bytes 6422528 | tf_op jit(solution)/shard_map/dot_general | solution.py:442
  84.9 3.7 %fusion.98 = bf16[512,704]{0,1:T(8,128)(2,1)S(1)} fusion(bf16[512,2048]{1,0:T(8,128)(2,1)S(1)} %bitcast.290, bf16[1,2,2048,704]{2,3,1,0:T(8,128)(2,1)} %param.32, f32[512,704]{0,1:T(8,128)S(1)} %fusion.16, f32[512]{0:T(512)S(1)} %mul.222), kind=kOutput, calls=%fused_computation.94 | convolution fusion | flops 1478918144 | bytes 7145472 | tf_op jit(solution)/shard_map/dot_general | solution.py:445
  92.7 4.3 %fusion.24 = f32[512,704]{0,1:T(8,128)S(1)} fusion(bf16[512,2048]{1,0:T(8,128)(2,1)} %bitcast.285, bf16[1,2,2048,704]{2,3,1,0:T(8,128)(2,1)} %param.31), kind=kOutput, calls=%fused_computation.38 | convolution fusion | flops 1476395008 | bytes 6422528 | tf_op jit(solution)/shard_map/dot_general | solution.py:442
  97.0 3.9 %fusion.92 = bf16[512,704]{0,1:T(8,128)(2,1)S(1)} fusion(bf16[512,2048]{1,0:T(8,128)(2,1)S(1)} %bitcast.286, bf16[1,2,2048,704]{2,3,1,0:T(8,128)(2,1)} %param.32, f32[512,704]{0,1:T(8,128)S(1)} %fusion.24, f32[512]{0:T(512)S(1)} %mul.217), kind=kOutput, calls=%fused_computation.92 | convolution fusion | flops 1478918144 | bytes 7145472 | tf_op jit(solution)/shard_map/dot_general | solution.py:445
  107.1 40.7 %shard_map.164 = bf16[128,2048]{1,0:T(8,128)(2,1)S(1)} custom-call(bf16[4,2,128,1024]{3,2,1,0:T(8,128)(2,1)S(1)} %bitcast.279, bf16[4,2,128,1024]{3,2,1,0:T(8,128)(2,1)S(1)} %bitcast.281), custom_call_target="tpu_custom_call" | custom-call | bytes 134217728 | tf_op jit(solution)/shard_map/pallas_call | solution.py:281
  150.0 14.4 %collective-permute-done = bf16[128,2048]{1,0:T(8,128)(2,1)S(1)} collective-permute-done((bf16[128,2048]{1,0:T(8,128)(2,1)}, bf16[128,2048]{1,0:T(8,128)(2,1)S(1)}, u32[]{:S(2)}, u32[]{:S(2)}) %collective-permute-start) | collective-permute-done | bytes 524320 | tf_op jit(solution)/shard_map/ppermute | solution.py:305
  165.8 3.2 %fusion.127 = bf16[16,8,8,128]{3,2,1,0:T(8,128)(2,1)S(1)} fusion(bf16[1,2048,1024]{2,1,0:T(8,128)(2,1)} %param.24, bf16[128,2048]{1,0:T(8,128)(2,1)S(1)} %get-tuple-element.14, f32[2048]{0:T(1024)S(1)} %bitcast.306, f32[128]{0:T(128)S(1)} %add_rsqrt_fusion.2), kind=kOutput, calls=%fused_computation.117 | convolution fusion | flops 538050560 | bytes 4989440 | tf_op jit(solution)/shard_map/dot_general | solution.py:394
  170.2 4.5 %fusion.107 = f32[128,8,896]{2,0,1:T(8,128)} fusion(bf16[1,8,128,512]{3,2,1,0:T(8,128)(2,1)S(1)} %copy-done.6, bf16[128,512]{1,0:T(8,128)(2,1)S(1)} %multiply_convert_fusion.2, bf16[768,512]{1,0:T(8,128)(2,1)} %get-tuple-element.17, bf16[16,8,8,128]{3,2,1,0:T(8,128)(2,1)S(1)} %fusion.127), kind=kOutput, calls=%fused_computation.99 | convolution fusion | flops 1076101120 | bytes 5898240 | tf_op jit(solution)/shard_map/thl,kl->thk/dot_general | solution.py:319
  174.7 6.8 %fusion.193 = (f32[128,8]{0,1:T(8,128)S(1)}, f32[128,8,896]{2,0,1:T(8,128)}) fusion(f32[128,8,896]{2,0,1:T(8,128)} %fusion.107, pred[128,896]{1,0:T(8,128)(4,1)S(1)} %copy-done.21), kind=kOutput, calls=%fused_computation.208 | output fusion | flops 6423423 | bytes 7458816 | tf_op jit(solution)/shard_map/sub | solution.py:326
  181.5 3.7 %fusion.125 = bf16[8,128,128]{1,2,0:T(8,128)(2,1)S(1)} fusion(f32[128,8,896]{2,0,1:T(8,128)} %get-tuple-element.38, f32[128,8]{0,1:T(8,128)S(1)} %get-tuple-element.37, bf16[1,8,512,128]{3,2,1,0:T(8,128)(2,1)S(1)} %copy-done.28, bf16[128,512]{1,0:T(8,128)(2,1)S(1)} %multiply_convert_fusion.2, bf16[768,512]{1,0:T(8,128)(2,1)S(1)} %copy-done.7), kind=kOutput, calls=%fused_computation.115 | convolution fusion | flops 1078067200 | bytes 5902336 | tf_op jit(solution)/shard_map/thl,hld->thd/dot_general | solution.py:407
  185.2 3.0 %multiply_reduce_fusion = (f32[128]{0:T(128)S(1)}, f32[128,2048]{1,0:T(8,128)S(1)}) fusion(bf16[128,1024]{0,1:T(8,128)(2,1)S(1)} %bitcast.301, bf16[1,1024,2048]{2,1,0:T(8,128)(2,1)} %param.27, bf16[128,2048]{1,0:T(8,128)(2,1)S(1)} %copy-done.4), kind=kOutput, calls=%fused_computation.138 | convolution fusion | flops 538443648 | bytes 6029824 | tf_op jit(solution)/shard_map/dot_general | solution.py:411
  188.4 35.8 %shard_map.165 = (bf16[4,2,128,2048]{3,2,1,0:T(8,128)(2,1)S(1)}, f32[4,2,16,128]{3,2,1,0:T(8,128)S(1)}) custom-call(bf16[128,2048]{1,0:T(8,128)(2,1)S(1)} %multiply_convert_fusion.own_ref, f32[16,128]{1,0:T(8,128)S(1)} %get-tuple-element.19.small_ref), custom_call_target="tpu_custom_call" | custom-call | bytes 134217728 | tf_op jit(solution)/shard_map/pallas_call | solution.py:156
  229.0 4.3 %fusion.14 = f32[512,704]{0,1:T(8,128)S(1)} fusion(bf16[512,2048]{1,0:T(8,128)(2,1)} %bitcast.291, bf16[1,2,2048,704]{2,3,1,0:T(8,128)(2,1)} %param.31), kind=kOutput, calls=%fused_computation.28 | convolution fusion | flops 1476395008 | bytes 6422528 | tf_op jit(solution)/shard_map/dot_general | solution.py:442
  233.3 3.9 %fusion.101 = bf16[512,704]{0,1:T(8,128)(2,1)S(1)} fusion(bf16[512,2048]{1,0:T(8,128)(2,1)S(1)} %bitcast.292, bf16[1,2,2048,704]{2,3,1,0:T(8,128)(2,1)} %param.32, f32[512,704]{0,1:T(8,128)S(1)} %fusion.14, f32[512]{0:T(512)S(1)} %mul.246), kind=kOutput, calls=%fused_computation.95 | convolution fusion | flops 1478918144 | bytes 7145472 | tf_op jit(solution)/shard_map/dot_general | solution.py:445
  240.3 4.3 %fusion.22 = f32[512,704]{0,1:T(8,128)S(1)} fusion(bf16[512,2048]{1,0:T(8,128)(2,1)} %bitcast.287, bf16[1,2,2048,704]{2,3,1,0:T(8,128)(2,1)} %param.31), kind=kOutput, calls=%fused_computation.36 | convolution fusion | flops 1476395008 | bytes 6422528 | tf_op jit(solution)/shard_map/dot_general | solution.py:442
  244.6 3.9 %fusion.95 = bf16[512,704]{0,1:T(8,128)(2,1)S(1)} fusion(bf16[512,2048]{1,0:T(8,128)(2,1)S(1)} %bitcast.288, bf16[1,2,2048,704]{2,3,1,0:T(8,128)(2,1)} %param.32, f32[512,704]{0,1:T(8,128)S(1)} %fusion.22, f32[512]{0:T(512)S(1)} %mul.241), kind=kOutput, calls=%fused_computation.93 | convolution fusion | flops 1478918144 | bytes 7145472 | tf_op jit(solution)/shard_map/dot_general | solution.py:445
  254.1 40.7 %shard_map.166 = bf16[128,2048]{1,0:T(8,128)(2,1)S(1)} custom-call(bf16[4,2,128,1024]{3,2,1,0:T(8,128)(2,1)S(1)} %bitcast.282, bf16[4,2,128,1024]{3,2,1,0:T(8,128)(2,1)S(1)} %bitcast.280), custom_call_target="tpu_custom_call" | custom-call | bytes 134217728 | tf_op jit(solution)/shard_map/pallas_call | solution.py:281
  (127 shorter events, 47.6 us)
Async XLA Ops:
  0.0 7.6 %copy-start = (bf16[1,2048,512]{2,1,0:T(8,128)(2,1)S(1)}, bf16[1,2048,512]{2,1,0:T(8,128)(2,1)}, u32[]{:S(2)}) copy-start(bf16[1,2048,512]{2,1,0:T(8,128)(2,1)} %param.28) | copy-start | bytes 6291460
  0.0 7.7 %copy-start.2 = (bf16[1,128,2048]{2,1,0:T(8,128)(2,1)S(1)}, bf16[1,128,2048]{2,1,0:T(8,128)(2,1)}, u32[]{:S(2)}) copy-start(bf16[1,128,2048]{2,1,0:T(8,128)(2,1)} %param.17) | copy-start | bytes 1572868
  0.0 7.7 %copy-start.22 = (f32[1,2048]{1,0:T(1,128)S(1)}, f32[1,2048]{1,0:T(1,128)}, u32[]{:S(2)}) copy-start(f32[1,2048]{1,0:T(1,128)} %param.23) | copy-start | bytes 24580
  4.4 5.1 %copy-start.17 = (bf16[2,1,1,768,512]{4,3,2,1,0:T(8,128)(2,1)S(1)}, bf16[2,1,1,768,512]{4,3,2,1,0:T(8,128)(2,1)}, u32[]{:S(2)}) copy-start(bf16[2,1,1,768,512]{4,3,2,1,0:T(8,128)(2,1)} %param.19) | copy-start | bytes 4718596
  8.9 6.3 %copy-start.5 = (bf16[1,8,128,512]{3,2,1,0:T(8,128)(2,1)S(1)}, bf16[1,8,128,512]{3,2,1,0:T(8,128)(2,1)}, u32[]{:S(2)}) copy-start(bf16[1,8,128,512]{3,2,1,0:T(8,128)(2,1)} %param.25) | copy-start | bytes 3145732
  19.6 6.8 %copy-start.8 = (bf16[768,512]{1,0:T(8,128)(2,1)S(1)}, bf16[768,512]{1,0:T(8,128)(2,1)}, u32[]{:S(2)}) copy-start(bf16[768,512]{1,0:T(8,128)(2,1)} %get-tuple-element.18) | copy-start | bytes 2359300
  30.4 39.9 %copy-start.26 = (s32[64]{0:T(128)S(1)}, s32[64]{0:T(128)}, u32[]{:S(2)}) copy-start(s32[64]{0:T(128)} %iota_add_fusion.1) | copy-start | bytes 772
  74.9 5.5 %copy-start.15 = (bf16[8,64,2048]{2,1,0:T(8,128)(2,1)S(1)}, bf16[8,64,2048]{2,1,0:T(8,128)(2,1)}, u32[]{:S(2)}) copy-start(bf16[8,64,2048]{2,1,0:T(8,128)(2,1)} %convolution_convert_fusion.2) | copy-start | bytes 6291460
  80.3 10.3 %copy-start.11 = (bf16[704,2048]{1,0:T(8,128)(2,1)}, bf16[704,2048]{1,0:T(8,128)(2,1)S(1)}, u32[]{:S(2)}) copy-start(bf16[704,2048]{1,0:T(8,128)(2,1)S(1)} %get-tuple-element.15) | copy-start | bytes 8650756
  92.7 4.3 %copy-start.13 = (bf16[8,64,2048]{2,1,0:T(8,128)(2,1)S(1)}, bf16[8,64,2048]{2,1,0:T(8,128)(2,1)}, u32[]{:S(2)}) copy-start(bf16[8,64,2048]{2,1,0:T(8,128)(2,1)} %convolution_convert_fusion.3) | copy-start | bytes 6291460
  97.0 3.9 %copy-start.9 = (bf16[704,2048]{1,0:T(8,128)(2,1)S(1)}, bf16[704,2048]{1,0:T(8,128)(2,1)}, u32[]{:S(2)}) copy-start(bf16[704,2048]{1,0:T(8,128)(2,1)} %get-tuple-element.16) | copy-start | bytes 8650756
  147.8 18.0 %copy-start.23 = (f32[1,2048]{1,0:T(1,128)S(1)}, f32[1,2048]{1,0:T(1,128)}, u32[]{:S(2)}) copy-start(f32[1,2048]{1,0:T(1,128)} %param.23) | copy-start | bytes 24580
  148.7 15.7 %collective-permute-start = (bf16[128,2048]{1,0:T(8,128)(2,1)}, bf16[128,2048]{1,0:T(8,128)(2,1)S(1)}, u32[]{:S(2)}, u32[]{:S(2)}) collective-permute-start(bf16[128,2048]{1,0:T(8,128)(2,1)} %add_convert_fusion.5), channel_id=1, source_target_pairs={{0,1},{2,3},{4,5},{6,7},{8,9},{10,11},{12,13},{14,15},{16,17},{18,... | collective-permute-start | bytes 1572872 | tf_op jit(solution)/shard_map/ppermute | solution.py:305
  165.7 3.8 %copy-start.3 = (bf16[128,2048]{1,0:T(8,128)(2,1)}, bf16[128,2048]{1,0:T(8,128)(2,1)S(1)}, u32[]{:S(2)}) copy-start(bf16[128,2048]{1,0:T(8,128)(2,1)S(1)} %get-tuple-element.14) | copy-start | bytes 1572868
  165.8 3.8 %copy-start.25 = (f32[1,512]{1,0:T(1,128)S(1)}, f32[1,512]{1,0:T(1,128)}, u32[]{:S(2)}) copy-start(f32[1,512]{1,0:T(1,128)} %param.29) | copy-start | bytes 6148
  170.2 4.5 %copy-start.21 = (pred[128,896]{1,0:T(8,128)(4,1)S(1)}, pred[128,896]{1,0:T(8,128)(4,1)}, u32[]{:S(2)}) copy-start(pred[128,896]{1,0:T(8,128)(4,1)} %get-tuple-element.25) | copy-start | bytes 344068
  174.7 6.8 %copy-start.7 = (bf16[768,512]{1,0:T(8,128)(2,1)S(1)}, bf16[768,512]{1,0:T(8,128)(2,1)}, u32[]{:S(2)}) copy-start(bf16[768,512]{1,0:T(8,128)(2,1)} %get-tuple-element.17) | copy-start | bytes 2359300
  174.7 6.8 %copy-start.28 = (bf16[1,8,512,128]{3,2,1,0:T(8,128)(2,1)S(1)}, bf16[1,8,512,128]{3,2,1,0:T(8,128)(2,1)}, u32[]{:S(2)}) copy-start(bf16[1,8,512,128]{3,2,1,0:T(8,128)(2,1)} %param.26) | copy-start | bytes 3145732
  181.5 3.7 %copy-start.4 = (bf16[128,2048]{1,0:T(8,128)(2,1)S(1)}, bf16[128,2048]{1,0:T(8,128)(2,1)}, u32[]{:S(2)}) copy-start(bf16[128,2048]{1,0:T(8,128)(2,1)} %copy-done.3) | copy-start | bytes 1572868
  229.0 4.3 %copy-start.16 = (bf16[8,64,2048]{2,1,0:T(8,128)(2,1)S(1)}, bf16[8,64,2048]{2,1,0:T(8,128)(2,1)}, u32[]{:S(2)}) copy-start(bf16[8,64,2048]{2,1,0:T(8,128)(2,1)} %convolution_convert_fusion) | copy-start | bytes 6291460
  233.3 3.9 %copy-start.12 = (bf16[704,2048]{1,0:T(8,128)(2,1)S(1)}, bf16[704,2048]{1,0:T(8,128)(2,1)}, u32[]{:S(2)}) copy-start(bf16[704,2048]{1,0:T(8,128)(2,1)} %copy-done.11) | copy-start | bytes 8650756
  240.3 4.3 %copy-start.14 = (bf16[8,64,2048]{2,1,0:T(8,128)(2,1)S(1)}, bf16[8,64,2048]{2,1,0:T(8,128)(2,1)}, u32[]{:S(2)}) copy-start(bf16[8,64,2048]{2,1,0:T(8,128)(2,1)} %convolution_convert_fusion.1) | copy-start | bytes 6291460
  244.6 3.9 %copy-start.10 = (bf16[704,2048]{1,0:T(8,128)(2,1)S(1)}, bf16[704,2048]{1,0:T(8,128)(2,1)}, u32[]{:S(2)}) copy-start(bf16[704,2048]{1,0:T(8,128)(2,1)} %get-tuple-element.16) | copy-start | bytes 8650756
  254.1 42.9 %copy-start.1 = (bf16[1,2048,512]{2,1,0:T(8,128)(2,1)S(1)}, bf16[1,2048,512]{2,1,0:T(8,128)(2,1)}, u32[]{:S(2)}) copy-start(bf16[1,2048,512]{2,1,0:T(8,128)(2,1)} %param.28) | copy-start | bytes 6291460
  (6 other events, 11.1 us)
where the time goes:
time: 303 us; the launch traced here: 297 us
  Pallas kernels  153 us (50%)
  matrix products  89.6 us (30%)
  other arithmetic  26.7 us (9%)
  waiting for transfers between devices  14.4 us (5%)
  local copies, waits for them, and re-layouts  10.9 us (4%)
    pallas_call x2, Pallas kernels, gather_sum(): pl.pallas_call(gather_sum_kernel, out_shape=jax.ShapeDtypeStruct((height,...  81.4 us
    pallas_call x2, Pallas kernels, spread(): pl.pallas_call(spread_kernel, out_shape=[jax.ShapeDtypeStruct((chips, pai...  72.1 us
    dot_general x4, matrix products, shards(): jnp.dot(rows_in, specialist_switch_factor[0, e], preferred_element_type=j...  17.4 us
    dot_general x4, matrix products, shards(): jnp.dot(rows_in, specialist_widen_factor[0, e], preferred_element_type=jn...  15.3 us
    ppermute x1, waiting for transfers between devices, shifted(): lax.ppermute(value, axis, [(source, source + steps) for source in range(i...  14.4 us
    sub x2, other arithmetic, attend(): expd = jnp.where(visible[:, None, :], jnp.exp(scores - row_max), 0.0)  13.5 us
    dot_general x8, matrix products, shards(): jnp.dot(hidden_list[e], specialist_contract_factor[0, e][:, c * chunk:(c...  11.1 us
    dot_general x2, matrix products, attend(): jnp.einsum('thl,kl->thk', q_lat, key_rows, preferred_element_type=jnp.flo...  9.01 us
  transfers between devices with their start and end apart: 1, of which 1 were waited for; matrix products, arithmetic and copies ran while one was open for 0% of the time, Pallas kernels for 0%

commit v1 on v0

v1 whole, which is shorter than its diff:
```python
import jax
import jax.numpy as jnp
from jax import lax
from jax.experimental import pallas as pl
from jax.experimental.pallas import tpu as pltpu
from jax.sharding import PartitionSpec as P


epsilon = 1e-06


MESH = pl.DeviceIdType.MESH
PIECES = 4
RETURN_PIECES = 4
NT = (((1,), (1,)), ((), ()))


def place_on_line():
    count = lax.axis_size("expert")
    pair = 2 if count % 2 == 0 else 1
    mine = lax.axis_index("expert")
    return count // pair, pair, mine, mine // pair, lax.rem(mine, pair)


def greet(chips, pair, mine, spot, side):
    barrier = pltpu.get_barrier_semaphore()

    def hello(other):
        pl.semaphore_signal(barrier, inc=1, device_id={"expert": other}, device_id_type=MESH)

    @pl.when(spot > 0)
    def _():
        hello(mine - pair)

    @pl.when(spot < chips - 1)
    def _():
        hello(mine + pair)

    if pair == 2:
        hello(mine + 1 - 2 * side)
    inner = (spot > 0) & (spot < chips - 1)

    @pl.when(inner)
    def _():
        pl.semaphore_wait(barrier, pair + 1)

    @pl.when(jnp.logical_not(inner))
    def _():
        pl.semaphore_wait(barrier, pair)


def remote(src, dst, send, recv, other):
    return pltpu.make_async_remote_copy(
        src_ref=src,
        dst_ref=dst,
        send_sem=send,
        recv_sem=recv,
        device_id={"expert": other},
        device_id_type=MESH,
    )


def visiting_order(k, spot, chips):
    low = jnp.minimum(spot, chips - 1 - spot)
    near = (k + 1) // 2
    around = spot + jnp.where(lax.rem(k, 2) == 0, near, -near)
    rest = jnp.where(spot < chips - 1 - spot, k, chips - 1 - k)
    return jnp.where(k <= 2 * low, around, rest)


def experts_kernel(
    own_ref,
    small_ref,
    gate_hbm,
    up_hbm,
    down_hbm,
    sum_ref,
    gate,
    up,
    down,
    rows_all,
    small_all,
    hidden,
    part,
    side_in,
    line_in,
    own_sem,
    weight_sem,
    line_send,
    line_recv,
    side_send,
    side_recv,
    give_send,
    give_recv,
    back_send,
    back_recv,
):
    chips, pair, mine, spot, side = place_on_line()
    height, width = own_ref.shape
    local = gate.shape[0]
    step = height // PIECES
    chunk = width // RETURN_PIECES
    sibling = mine + 1 - 2 * side
    at_end = (spot == 0) | (spot == chips - 1)

    loads = []
    for index, (source, target) in enumerate(((gate_hbm, gate), (up_hbm, up), (down_hbm, down))):
        for e in range(local):
            loads.append(
                pltpu.make_async_copy(source.at[e], target.at[e], weight_sem.at[index, e])
            )

    def rows(block, core, piece):
        if piece == PIECES:
            return small_all.at[block, core]
        first = pl.multiple_of(core * height + piece * step, step)
        return rows_all.at[block, pl.ds(first, step)]

    def origin(block, piece):
        if block is not None:
            return rows(block, side, piece)
        return small_ref if piece == PIECES else own_ref.at[pl.ds(piece * step, step)]

    def line_copy(block, piece, way):
        where = spot if block is None else block
        direction = 0 if way > 0 else 1
        return remote(
            origin(block, piece),
            rows(where, side, piece),
            line_send.at[direction, where, piece],
            line_recv.at[where, piece],
            mine + way * pair,
        )

    def side_copy(block, piece):
        where = spot if block is None else block
        return remote(
            origin(block, piece),
            rows(where, side, piece),
            side_send.at[where, piece],
            side_recv.at[where, piece],
            sibling,
        )

    def onward(block, piece, way, act):
        @pl.when((spot < chips - 1) if way > 0 else (spot > 0))
        def _():
            act(line_copy(block, piece, way))

    def passing(far, act):
        for piece in range(PIECES + 1):
            for way in (1, -1):
                block = spot - way * far

                @pl.when((block >= 0) if way > 0 else (block < chips))
                def _():
                    act(block, piece, way)

    def give_copy(block, piece):
        return remote(
            part.at[block, 1 - side, piece],
            side_in.at[block, piece],
            give_send.at[block, piece],
            give_recv.at[block, piece],
            sibling,
        )

    def back_copy(block, piece, way):
        direction = (1 - way) // 2
        return remote(
            part.at[block, side, piece],
            line_in.at[direction, block, piece],
            back_send.at[block, piece],
            back_recv.at[direction, block, piece],
            mine + way * pair,
        )

    def wide(value):
        return value.astype(jnp.float32)

    def combine(block, piece, way, from_line):
        give_copy(block, piece).wait_recv()
        value = wide(part[block, side, piece]) + wide(side_in[block, piece])
        if from_line:
            back_copy(block, piece, way).wait_recv()
            value = value + wide(line_in[(1 - way) // 2, block, piece])
        part[block, side, piece] = value.astype(part.dtype)
        back_copy(block, piece, way).start()

    greet(chips, pair, mine, spot, side)
    for piece in (PIECES, *range(PIECES)):
        for way in (1, -1):
            onward(None, piece, way, lambda copy: copy.start())
        side_copy(None, piece).start()
    keep = pltpu.make_async_copy(
        own_ref, rows_all.at[spot, pl.ds(pl.multiple_of(side * height, height), height)], own_sem.at[0]
    )
    keep.start()
    keep_small = pltpu.make_async_copy(small_ref, small_all.at[spot, side], own_sem.at[1])
    keep_small.start()
    for load in loads:
        load.start()
    keep.wait()
    keep_small.wait()
    for load in loads:
        load.wait()

    def visit(k, carry):
        block = visiting_order(k, spot, chips)
        way = jnp.where(block > spot, 1, -1)
        outward = at_end & (k > 0)
        for piece in range(PIECES + 1):
            side_copy(block, piece).wait_recv()
        values = rows_all[block]
        for e in range(local):
            chosen_expert = mine * local + e
            columns = []
            for core in range(pair):
                table = small_all[block, core]
                here = lax.broadcasted_iota(jnp.int32, table.shape, 0) == chosen_expert
                row = jnp.sum(jnp.where(here, table, 0.0), axis=0, keepdims=True)
                columns.append(jnp.broadcast_to(row, (height, height)).T[:, :1])
            share = jnp.concatenate(columns, axis=0)
            gated = lax.dot_general(values, gate[e], NT, preferred_element_type=jnp.float32)
            upped = lax.dot_general(values, up[e], NT, preferred_element_type=jnp.float32)
            hidden[e] = (gated * jax.nn.sigmoid(gated) * upped * share).astype(hidden.dtype)
        for piece in range(RETURN_PIECES):
            total = None
            for e in range(local):
                term = jnp.dot(
                    hidden[e],
                    down[e, :, piece * chunk : (piece + 1) * chunk],
                    preferred_element_type=jnp.float32,
                )
                total = term if total is None else total + term
            total = total.astype(part.dtype)
            for core in range(pair):
                part[block, core, piece] = total[core * height : (core + 1) * height]
            give_copy(block, piece).start()
            if piece > 0:

                @pl.when(outward)
                def _():
                    combine(block, piece - 1, way, False)

        @pl.when(outward)
        def _():
            combine(block, RETURN_PIECES - 1, way, False)

        @pl.when(k < chips - 1)
        def _():
            def receive(block, piece, way):
                line_copy(block, piece, way).wait_recv()
                onward(block, piece, way, lambda copy: copy.start())
                side_copy(block, piece).start()

            passing(k + 1, receive)

        return carry

    lax.fori_loop(0, chips, visit, 0)

    left_first = 2 * spot <= chips - 1

    def relay(a, carry):
        for piece in range(RETURN_PIECES):
            for turn in range(2):
                way = jnp.where(left_first, 1 - 2 * turn, 2 * turn - 1)
                block = jnp.where(way > 0, a, chips - 1 - a)
                valid = jnp.where(way > 0, block > spot, block < spot) & jnp.logical_not(at_end)

                @pl.when(valid)
                def _():
                    combine(block, piece, way, True)

        return carry

    lax.fori_loop(1, chips, relay, 0)
    for piece in range(RETURN_PIECES):
        give_copy(spot, piece).wait_recv()
        columns = pl.ds(piece * chunk, chunk)
        sum_ref[:, columns] = wide(part[spot, side, piece]) + wide(side_in[spot, piece])
        for way in (1, -1):

            @pl.when((spot > 0) if way > 0 else (spot < chips - 1))
            def _():
                back_copy(spot, piece, way).wait_recv()
                sum_ref[:, columns] += wide(line_in[(1 - way) // 2, spot, piece])

    for piece in range(PIECES + 1):
        for way in (1, -1):
            onward(None, piece, way, lambda copy: copy.wait_send())
        side_copy(None, piece).wait_send()

    def settle(far, carry):
        def sent(block, piece, way):
            onward(block, piece, way, lambda copy: copy.wait_send())
            side_copy(block, piece).wait_send()

        passing(far, sent)
        return carry

    lax.fori_loop(1, chips, settle, 0)

    def settle_back(block, carry):
        for piece in range(RETURN_PIECES):
            give_copy(block, piece).wait_send()

            @pl.when(block != spot)
            def _():
                back_copy(block, piece, jnp.where(block > spot, 1, -1)).wait_send()

        return carry

    lax.fori_loop(0, chips, settle_back, 0)


def experts(own, small, gate, up, down):
    count = lax.axis_size("expert")
    pair = 2
    chips = count // pair
    height, width = own.shape
    local, inner = down.shape[:2]
    kind = own.dtype
    chunk = width // RETURN_PIECES
    blocks = chips * pair * height * width * 2
    weights = 3 * local * inner * width * 2
    dma = pltpu.SemaphoreType.DMA
    hbm = pl.BlockSpec(memory_space=pl.ANY)
    vmem = pl.BlockSpec(memory_space=pltpu.VMEM)
    return pl.pallas_call(
        experts_kernel,
        out_shape=jax.ShapeDtypeStruct((height, width), jnp.float32),
        in_specs=[vmem, vmem, hbm, hbm, hbm],
        out_specs=vmem,
        scratch_shapes=[
            pltpu.VMEM((local, inner, width), kind),
            pltpu.VMEM((local, inner, width), kind),
            pltpu.VMEM((local, inner, width), kind),
            pltpu.VMEM((chips, pair * height, width), kind),
            pltpu.VMEM((chips, pair) + small.shape, small.dtype),
            pltpu.VMEM((local, pair * height, inner), kind),
            pltpu.VMEM((chips, pair, RETURN_PIECES, height, chunk), kind),
            pltpu.VMEM((chips, RETURN_PIECES, height, chunk), kind),
            pltpu.VMEM((2, chips, RETURN_PIECES, height, chunk), kind),
            dma((2,)),
            dma((3, local)),
            dma((2, chips, PIECES + 1)),
            dma((chips, PIECES + 1)),
            dma((chips, PIECES + 1)),
            dma((chips, PIECES + 1)),
            dma((chips, RETURN_PIECES)),
            dma((chips, RETURN_PIECES)),
            dma((chips, RETURN_PIECES)),
            dma((2, chips, RETURN_PIECES)),
        ],
        compiler_params=pltpu.CompilerParams(
            collective_id=0, has_side_effects=True, vmem_limit_bytes=4 * blocks + weights + 12 * 2**20
        ),
        cost_estimate=pl.CostEstimate(
            flops=2 * weights * blocks // (width * 4), bytes_accessed=32 * blocks, transcendentals=0
        ),
    )(own, small, gate, up, down)


def shifted(value, axis, steps):
    count = lax.axis_size(axis)
    initial, last = (max(0, -steps), min(count, count - steps))
    return lax.ppermute(value, axis, [(source, source + steps) for source in range(initial, last)])


def row_norm(values, gain_row):
    return (
        values * lax.rsqrt(jnp.mean(values * values, axis=-1, keepdims=True) + epsilon) * gain_row
    )


def attend(q_lat, cache_rows, new_rows, length, score_scale):
    piece_list = q_lat.shape[0]
    context = cache_rows.shape[0]
    key_rows = jnp.concatenate([cache_rows, new_rows], axis=0)
    scores = (
        jnp.einsum("thl,kl->thk", q_lat, key_rows, preferred_element_type=jnp.float32) * score_scale
    )
    position = lax.broadcasted_iota(jnp.int32, (piece_list, context + piece_list), 1)
    query_pos = lax.broadcasted_iota(jnp.int32, (piece_list, context + piece_list), 0)
    visible = jnp.where(position < context, position < length, position - context <= query_pos)
    scores = jnp.where(visible[:, None, :], scores, -jnp.inf)
    row_max = jnp.max(scores, axis=-1, keepdims=True)
    expd = jnp.where(visible[:, None, :], jnp.exp(scores - row_max), 0.0)
    attention = (expd / jnp.sum(expd, axis=-1, keepdims=True)).astype(jnp.bfloat16)
    return jnp.einsum(
        "thk,kl->thl", attention, key_rows, preferred_element_type=jnp.float32
    ).astype(jnp.bfloat16)


def shards(
    opening_residual,
    incoming_residual,
    stored_summaries,
    stored_counts,
    picked_specialists,
    chooser_mixing_share,
    mixing_scale_factor,
    asking_projection,
    summary_lookup_factor,
    summary_content_factor,
    merging_projection,
    compress_projection,
    summary_scale_factor,
    specialist_scale_factor,
    specialist_switch_factor,
    specialist_widen_factor,
    specialist_contract_factor,
):
    segment_ordinal = lax.axis_index("section")
    section_count = lax.axis_size("section")
    sources = lax.axis_size("expert")
    tick_count = stored_summaries.shape[0]
    piece_list = opening_residual.shape[1]
    inner_feature_midcount = opening_residual.shape[2]
    full_width = mixing_scale_factor.shape[1]
    local_heads = summary_lookup_factor.shape[1]
    head_size = summary_lookup_factor.shape[2]
    top_count = picked_specialists.shape[3]
    expert_local = specialist_switch_factor.shape[1]
    score_scale = head_size ** (-0.5)
    expert_ids = lax.broadcasted_iota(jnp.int32, (1, 1, 1, expert_local * sources), 3)
    shares_dense = jnp.sum(
        jnp.where(
            picked_specialists[:, 0][..., None] == expert_ids,
            chooser_mixing_share[:, 0][..., None],
            0.0,
        ),
        axis=2,
    )
    shares_dense = jnp.swapaxes(shares_dense, 1, 2)
    outputs = []
    present_carry = opening_residual[0]
    section_out = present_carry
    for step_index in range(tick_count):
        if step_index > 0:
            handed = shifted(section_out, "section", 1)
            present_carry = jnp.where(
                segment_ordinal == 0, incoming_residual[step_index - 1], handed
            )
        micro_index = step_index - segment_ordinal + section_count - 1
        length = lax.dynamic_index_in_dim(stored_counts[:, 0], micro_index, 0, keepdims=False)
        full_rows = lax.all_gather(present_carry, "tensor", axis=1, tiled=True)
        normed = row_norm(full_rows.astype(jnp.float32), mixing_scale_factor[0]).astype(
            jnp.bfloat16
        )
        queries = jnp.dot(normed, asking_projection[0], preferred_element_type=jnp.float32).astype(
            jnp.bfloat16
        )
        queries = queries.reshape(piece_list, local_heads, head_size)
        q_lat = jnp.einsum(
            "thd,hdl->thl", queries, summary_lookup_factor[0], preferred_element_type=jnp.float32
        ).astype(jnp.bfloat16)
        latent_part = jnp.dot(normed, compress_projection[0], preferred_element_type=jnp.float32)
        latent_raw = lax.all_gather(
            latent_part.astype(jnp.bfloat16), "tensor", axis=1, tiled=True
        ).astype(latent_part.dtype)
        new_latent = row_norm(latent_raw, summary_scale_factor[0]).astype(jnp.bfloat16)
        o_lat = attend(q_lat, stored_summaries[step_index, 0, 0], new_latent, length, score_scale)
        heads_out = jnp.einsum(
            "thl,hld->thd", o_lat, summary_content_factor[0], preferred_element_type=jnp.float32
        ).astype(jnp.bfloat16)
        heads_out = heads_out.reshape(piece_list, local_heads * head_size)
        head_terms = jnp.dot(heads_out, merging_projection[0], preferred_element_type=jnp.float32)
        residual = present_carry.astype(jnp.float32) + lax.psum_scatter(
            head_terms.astype(jnp.bfloat16), "tensor", scatter_dimension=1, tiled=True
        ).astype(jnp.float32)
        squares = lax.psum(jnp.sum(residual * residual, axis=1), "tensor")
        moe_input = (
            residual
            * lax.rsqrt(squares / full_width + epsilon)[:, None]
            * specialist_scale_factor[0]
        ).astype(jnp.bfloat16)
        whole_rows = lax.all_gather(moe_input, "tensor", axis=1, tiled=True)
        routed = experts(
            whole_rows,
            shares_dense[step_index],
            jnp.swapaxes(specialist_switch_factor[0], 1, 2),
            jnp.swapaxes(specialist_widen_factor[0], 1, 2),
            specialist_contract_factor[0],
        )
        if lax.axis_size("tensor") > 1:
            routed = lax.psum_scatter(
                routed.astype(jnp.bfloat16), "tensor", scatter_dimension=1, tiled=True
            ).astype(jnp.float32)
        section_out = (residual + routed).astype(jnp.bfloat16)
        outputs.append(section_out)
    return jnp.stack(outputs)[:, None]


def solution(mesh):
    in_specs = (
        P("section", ("groups", "expert"), "tensor"),
        P(None, ("groups", "expert"), "tensor"),
        P(None, "section", ("groups", "expert"), None, None),
        P(None, ("groups", "expert")),
        P(None, "section", ("groups", "expert"), None),
        P(None, "section", ("groups", "expert"), None),
        P("section", None),
        P("section", None, "tensor"),
        P("section", "tensor", None, None),
        P("section", "tensor", None, None),
        P("section", "tensor", None),
        P("section", None, "tensor"),
        P("section", None),
        P("section", "tensor"),
        P("section", "expert", None, "tensor"),
        P("section", "expert", None, "tensor"),
        P("section", "expert", "tensor", None),
    )
    out_specs = P(None, "section", ("groups", "expert"), "tensor")
    return jax.shard_map(shards, mesh=mesh, in_specs=in_specs, out_specs=out_specs, check_vma=False)
```

time: 303 us -> 224 us (0.74)
  matrix products: 89.6 us -> 34.7 us
  Pallas kernels: 153 us -> 139 us
    dot_general x30 -> x0, matrix products: 58.6 us -> none  [the longest x4 17.4 us: shards(): jnp.dot(rows_in, specialist_switch_factor[0, e], preferred_element_type=j...]
    pallas_call x4 -> x2, Pallas kernels: 153 us -> 139 us  [experts(): pl.pallas_call(experts_kernel, out_shape=jax.ShapeDtypeStruct((height, wi...]
    squeeze x2 -> x1, local copies, waits for them, and re-layouts: 5.45 us -> 0.01 us  [shards(): shares_dense[step_index]]
    unnamed x62 -> x28, local copies, waits for them, and re-layouts: 3.24 us -> 6.71 us
where the time goes in v1:
time: 224 us; the launch traced here: 221 us
  Pallas kernels  139 us (62%)
  matrix products  34.7 us (15%)
  other arithmetic  24.1 us (11%)
  waiting for transfers between devices  12.4 us (6%)
  local copies, waits for them, and re-layouts  8.37 us (4%)
    pallas_call x2, Pallas kernels, experts(): pl.pallas_call(experts_kernel, out_shape=jax.ShapeDtypeStruct((height, wi...  139 us
    sub x2, other arithmetic, attend(): expd = jnp.where(visible[:, None, :], jnp.exp(scores - row_max), 0.0)  14 us
    ppermute x1, waiting for transfers between devices, shifted(): lax.ppermute(value, axis, [(source, source + steps) for source in range(i...  12.4 us
    dot_general x2, matrix products, attend(): jnp.einsum('thl,kl->thk', q_lat, key_rows, preferred_element_type=jnp.flo...  9.57 us
    dot_general x2, matrix products, shards(): jnp.einsum('thl,hld->thd', o_lat, summary_content_factor[0], preferred_el...  9.51 us
    dot_general x2, matrix products, shards(): jnp.dot(normed, asking_projection[0], preferred_element_type=jnp.float32)  7.63 us
    unnamed x28, local copies, waits for them, and re-layouts  6.71 us
    dot_general x2, matrix products, shards(): jnp.dot(heads_out, merging_projection[0], preferred_element_type=jnp.floa...  6.21 us
  transfers between devices with their start and end apart: 1, of which 1 were waited for; matrix products, arithmetic and copies ran while one was open for 0% of the time, Pallas kernels for 0%

profile of v1, /device:TPU:14, one launch (start us, length us, event | category | flops | bytes accessed | tf_op | source)
XLA Modules:
  0.0 220.8 jit_solution(3436091429063048057)
XLA Ops:
  1.2 1.2 fusion.77
  3.9 3.9 %fusion.62 = bf16[16,8,8,128]{3,2,1,0:T(8,128)(2,1)} fusion(bf16[1,2048,1024]{2,1,0:T(8,128)(2,1)} %param.24, bf16[1,128,2048]{2,1,0:T(8,128)(2,1)} %param.17, f32[2048]{0:T(1024)} %bitcast.158, f32[128]{0:T(128)S(1)} %add_rsqrt_fusion.5), kind=kOutput, calls=%fused_computation.56 | convolution fusion | flops 538050560 | bytes 4989440 | tf_op jit(solution)/shard_map/dot_general | solution.py:453
  7.8 1.2 multiply_reduce_fusion.3
  9.5 1.0 slice_bitcast_fusion
  11.2 1.4 iota_compare_fusion.2
  12.6 1.1 multiply_convert_fusion.3
  13.6 1.5 fusion.91
  15.1 4.9 %fusion.45 = f32[128,8,896]{2,0,1:T(8,128)} fusion(bf16[1,8,128,512]{3,2,1,0:T(8,128)(2,1)} %param.25, bf16[128,512]{1,0:T(8,128)(2,1)S(1)} %multiply_convert_fusion.3, bf16[768,512]{1,0:T(8,128)(2,1)} %get-tuple-element.8, bf16[16,8,8,128]{3,2,1,0:T(8,128)(2,1)} %fusion.62), kind=kOutput, calls=%fused_computation.43 | convolution fusion | flops 1076101120 | bytes 5898240 | tf_op jit(solution)/shard_map/thl,kl->thk/dot_general | solution.py:383
  20.0 7.3 %fusion.115 = (f32[128,8]{0,1:T(8,128)}, f32[128,8,896]{2,0,1:T(8,128)}) fusion(f32[128,8,896]{2,0,1:T(8,128)} %fusion.45, pred[128,896]{1,0:T(8,128)(4,1)} %get-tuple-element.12), kind=kOutput, calls=%fused_computation.122 | output fusion | flops 6423423 | bytes 7458816 | tf_op jit(solution)/shard_map/sub | solution.py:390
  27.3 4.9 %fusion.58 = bf16[8,128,128]{1,2,0:T(8,128)(2,1)} fusion(f32[128,8,896]{2,0,1:T(8,128)} %get-tuple-element.18, f32[128,8]{0,1:T(8,128)} %get-tuple-element.17, bf16[1,8,512,128]{3,2,1,0:T(8,128)(2,1)} %param.26, bf16[128,512]{1,0:T(8,128)(2,1)S(1)} %multiply_convert_fusion.3, bf16[768,512]{1,0:T(8,128)(2,1)} %get-tuple-element.8), kind=kOutput, calls=%fused_computation.54 | convolution fusion | flops 1078067200 | bytes 5902336 | tf_op jit(solution)/shard_map/thl,hld->thd/dot_general | solution.py:466
  32.2 3.1 %multiply_reduce_fusion.1 = (f32[128]{0:T(128)S(1)}, f32[128,2048]{1,0:T(8,128)S(1)}) fusion(bf16[128,1024]{0,1:T(8,128)(2,1)} %bitcast.156, bf16[1,1024,2048]{2,1,0:T(8,128)(2,1)} %param.27, bf16[1,128,2048]{2,1,0:T(8,128)(2,1)S(1)} %copy-done.3), kind=kOutput, calls=%fused_computation.77 | convolution fusion | flops 538443648 | bytes 6029824 | tf_op jit(solution)/shard_map/dot_general | solution.py:470
  35.5 2.6 %copy-done.1 = bf16[1,2,2048,704]{2,3,1,0:T(8,128)(2,1)S(1)} copy-done((bf16[1,2,2048,704]{2,3,1,0:T(8,128)(2,1)S(1)}, bf16[1,2,2048,704]{2,3,1,0:T(8,128)(2,1)}, u32[]{:S(2)}) %copy-start.1) | copy-done | bytes 5767192
  38.1 69.9 %shard_map.163 = f32[128,2048]{1,0:T(8,128)S(1)} custom-call(bf16[128,2048]{1,0:T(8,128)(2,1)S(1)} %multiply_convert_fusion.1.own_ref, f32[16,128]{1,0:T(8,128)S(1)} %get-tuple-element.10.small_ref, bf16[2,704,2048]{2,1,0:T(8,128)(2,1)S(1)} %bitcast.152, bf16[2,704,2048]{2,1,0:T(8,128)(2,1)} %bitcast.168, bf16[2,704,2048]{2,1,0:T(8,128)(2,1)} %bitcast.170), custom_call_target="tpu_custom_call" | custom-call | flops 17716740096 | bytes 134217728 | tf_op jit(solution)/shard_map/pallas_call | solution.py:331
  108.1 1.5 collective-permute-start
  109.7 12.4 %collective-permute-done = bf16[128,2048]{1,0:T(8,128)(2,1)} collective-permute-done((bf16[128,2048]{1,0:T(8,128)(2,1)S(1)}, bf16[128,2048]{1,0:T(8,128)(2,1)}, u32[]{:S(2)}, u32[]{:S(2)}) %collective-permute-start) | collective-permute-done | bytes 524320 | tf_op jit(solution)/shard_map/ppermute | solution.py:369
  122.1 1.5 fusion.80
  123.6 3.7 %fusion.59 = bf16[16,8,8,128]{3,2,1,0:T(8,128)(2,1)} fusion(bf16[1,2048,1024]{2,1,0:T(8,128)(2,1)} %param.24, bf16[128,2048]{1,0:T(8,128)(2,1)S(1)} %get-tuple-element.6, f32[2048]{0:T(1024)S(1)} %bitcast.160, f32[128]{0:T(128)S(1)} %add_rsqrt_fusion.2), kind=kOutput, calls=%fused_computation.55 | convolution fusion | flops 538050560 | bytes 4989440 | tf_op jit(solution)/shard_map/dot_general | solution.py:453
  128.0 4.7 %fusion.47 = f32[128,8,896]{2,0,1:T(8,128)} fusion(bf16[1,8,128,512]{3,2,1,0:T(8,128)(2,1)} %param.25, bf16[128,512]{1,0:T(8,128)(2,1)S(1)} %multiply_convert_fusion.2, bf16[768,512]{1,0:T(8,128)(2,1)S(1)} %get-tuple-element.7, bf16[16,8,8,128]{3,2,1,0:T(8,128)(2,1)} %fusion.59), kind=kOutput, calls=%fused_computation.45 | convolution fusion | flops 1076101120 | bytes 5898240 | tf_op jit(solution)/shard_map/thl,kl->thk/dot_general | solution.py:383
  132.6 6.7 %fusion.116 = (f32[128,8]{0,1:T(8,128)S(1)}, f32[128,8,896]{2,0,1:T(8,128)}) fusion(f32[128,8,896]{2,0,1:T(8,128)} %fusion.47, pred[128,896]{1,0:T(8,128)(4,1)} %get-tuple-element.11), kind=kOutput, calls=%fused_computation.123 | output fusion | flops 6423423 | bytes 7458816 | tf_op jit(solution)/shard_map/sub | solution.py:390
  139.4 4.6 %fusion.57 = bf16[8,128,128]{1,2,0:T(8,128)(2,1)} fusion(f32[128,8,896]{2,0,1:T(8,128)} %get-tuple-element.24, f32[128,8]{0,1:T(8,128)S(1)} %get-tuple-element.23, bf16[1,8,512,128]{3,2,1,0:T(8,128)(2,1)} %param.26, bf16[128,512]{1,0:T(8,128)(2,1)S(1)} %multiply_convert_fusion.2, bf16[768,512]{1,0:T(8,128)(2,1)S(1)} %get-tuple-element.7), kind=kOutput, calls=%fused_computation.53 | convolution fusion | flops 1078067200 | bytes 5902336 | tf_op jit(solution)/shard_map/thl,hld->thd/dot_general | solution.py:466
  144.0 3.1 %multiply_reduce_fusion = (f32[128]{0:T(128)S(1)}, f32[128,2048]{1,0:T(8,128)S(1)}) fusion(bf16[128,1024]{0,1:T(8,128)(2,1)} %bitcast.155, bf16[1,1024,2048]{2,1,0:T(8,128)(2,1)} %param.27, bf16[128,2048]{1,0:T(8,128)(2,1)S(1)} %get-tuple-element.6), kind=kOutput, calls=%fused_computation.74 | convolution fusion | flops 538443648 | bytes 6029824 | tf_op jit(solution)/shard_map/dot_general | solution.py:470
  147.3 2.6 %copy-done.2 = bf16[1,2,2048,704]{2,3,1,0:T(8,128)(2,1)S(1)} copy-done((bf16[1,2,2048,704]{2,3,1,0:T(8,128)(2,1)S(1)}, bf16[1,2,2048,704]{2,3,1,0:T(8,128)(2,1)}, u32[]{:S(2)}) %copy-start.2) | copy-done | bytes 5767192
  149.9 69.6 %shard_map.164 = f32[128,2048]{1,0:T(8,128)S(1)} custom-call(bf16[128,2048]{1,0:T(8,128)(2,1)S(1)} %multiply_convert_fusion.own_ref, f32[16,128]{1,0:T(8,128)S(1)} %get-tuple-element.9.small_ref, bf16[2,704,2048]{2,1,0:T(8,128)(2,1)S(1)} %bitcast.153, bf16[2,704,2048]{2,1,0:T(8,128)(2,1)} %bitcast.169, bf16[2,704,2048]{2,1,0:T(8,128)(2,1)} %bitcast.171), custom_call_target="tpu_custom_call" | custom-call | flops 17716740096 | bytes 134217728 | tf_op jit(solution)/shard_map/pallas_call | solution.py:331
  219.7 1.1 maximum_bitcast_fusion
  (45 shorter events, 5.0 us)
Async XLA Ops:
  0.0 7.8 %copy-start = (bf16[1,2048,512]{2,1,0:T(8,128)(2,1)S(1)}, bf16[1,2048,512]{2,1,0:T(8,128)(2,1)}, u32[]{:S(2)}) copy-start(bf16[1,2048,512]{2,1,0:T(8,128)(2,1)} %param.28) | copy-start | bytes 6291460
  0.0 7.8 %copy-start.3 = (bf16[1,128,2048]{2,1,0:T(8,128)(2,1)S(1)}, bf16[1,128,2048]{2,1,0:T(8,128)(2,1)}, u32[]{:S(2)}) copy-start(bf16[1,128,2048]{2,1,0:T(8,128)(2,1)} %param.17) | copy-start | bytes 1572868
  0.0 7.8 %copy-start.7 = (f32[1,2048]{1,0:T(1,128)S(1)}, f32[1,2048]{1,0:T(1,128)}, u32[]{:S(2)}) copy-start(f32[1,2048]{1,0:T(1,128)} %param.23) | copy-start | bytes 24580
  3.9 5.7 %copy-start.6 = (bf16[2,1,1,768,512]{4,3,2,1,0:T(8,128)(2,1)S(1)}, bf16[2,1,1,768,512]{4,3,2,1,0:T(8,128)(2,1)}, u32[]{:S(2)}) copy-start(bf16[2,1,1,768,512]{4,3,2,1,0:T(8,128)(2,1)} %param.19) | copy-start | bytes 4718596
  7.8 2.7 %copy-start.12 = (s32[3,1]{0,1:T(1,128)S(1)}, s32[3,1]{0,1:T(1,128)}, u32[]{:S(2)}) copy-start(s32[3,1]{0,1:T(1,128)} %param.20) | copy-start | bytes 40
  32.2 3.1 %copy-start.9 = (f32[1,2048]{1,0:T(1,128)S(1)}, f32[1,2048]{1,0:T(1,128)}, u32[]{:S(2)}) copy-start(f32[1,2048]{1,0:T(1,128)} %param.30) | copy-start | bytes 24580
  35.5 2.6 %copy-start.1 = (bf16[1,2,2048,704]{2,3,1,0:T(8,128)(2,1)S(1)}, bf16[1,2,2048,704]{2,3,1,0:T(8,128)(2,1)}, u32[]{:S(2)}) copy-start(bf16[1,2,2048,704]{2,3,1,0:T(8,128)(2,1)} %param.31) | copy-start | bytes 17301508
  108.0 15.6 %copy-start.8 = (f32[1,2048]{1,0:T(1,128)S(1)}, f32[1,2048]{1,0:T(1,128)}, u32[]{:S(2)}) copy-start(f32[1,2048]{1,0:T(1,128)} %param.23) | copy-start | bytes 24580
  108.1 1.5 copy-start.4
  108.1 14.0 %collective-permute-start = (bf16[128,2048]{1,0:T(8,128)(2,1)S(1)}, bf16[128,2048]{1,0:T(8,128)(2,1)}, u32[]{:S(2)}, u32[]{:S(2)}) collective-permute-start(bf16[128,2048]{1,0:T(8,128)(2,1)S(1)} %add_convert_fusion.1), channel_id=1, source_target_pairs={{0,1},{2,3},{4,5},{6,7},{8,9},{10,11},{12,13},{14,15},{16,17},{18,... | collective-permute-start | bytes 1572872 | tf_op jit(solution)/shard_map/ppermute | solution.py:369
  123.6 4.3 %copy-start.11 = (f32[1,512]{1,0:T(1,128)S(1)}, f32[1,512]{1,0:T(1,128)}, u32[]{:S(2)}) copy-start(f32[1,512]{1,0:T(1,128)} %param.29) | copy-start | bytes 6148
  144.0 3.1 %copy-start.10 = (f32[1,2048]{1,0:T(1,128)S(1)}, f32[1,2048]{1,0:T(1,128)}, u32[]{:S(2)}) copy-start(f32[1,2048]{1,0:T(1,128)} %param.30) | copy-start | bytes 24580
  147.3 2.6 %copy-start.2 = (bf16[1,2,2048,704]{2,3,1,0:T(8,128)(2,1)S(1)}, bf16[1,2,2048,704]{2,3,1,0:T(8,128)(2,1)}, u32[]{:S(2)}) copy-start(bf16[1,2,2048,704]{2,3,1,0:T(8,128)(2,1)} %param.31) | copy-start | bytes 17301508
  149.9 69.8 %copy-start.5 = (bf16[128,2048]{1,0:T(8,128)(2,1)S(1)}, bf16[128,2048]{1,0:T(8,128)(2,1)}, u32[]{:S(2)}) copy-start(bf16[128,2048]{1,0:T(8,128)(2,1)} %copy-done.4) | copy-start | bytes 1572868

commit v2 on v1

--- a/solution.py
+++ b/solution.py
@@ -363,6 +363,710 @@
     )(own, small, gate, up, down)
 
 
+HALVES = 2
+
+
+def relay_kernel(
+    lengths,
+    shares_ref,
+    mixing_gain,
+    latent_gain,
+    expert_gain,
+    opening_hbm,
+    incoming_hbm,
+    stored_hbm,
+    asking_hbm,
+    compress_hbm,
+    lookup_hbm,
+    content_hbm,
+    merging_hbm,
+    gate_hbm,
+    up_hbm,
+    down_hbm,
+    out_hbm,
+    asking,
+    compress,
+    lookup,
+    content,
+    merging,
+    gate,
+    up,
+    down,
+    keys,
+    inputs,
+    residual,
+    q_lat,
+    rows_all,
+    small_all,
+    hidden,
+    part,
+    side_in,
+    line_in,
+    results,
+    input_sem,
+    load_sem,
+    gate_sem,
+    key_sem,
+    out_sem,
+    small_sem,
+    line_send,
+    line_recv,
+    side_send,
+    side_recv,
+    small_line_send,
+    small_line_recv,
+    small_side_send,
+    small_side_recv,
+    give_send,
+    give_recv,
+    back_send,
+    back_recv,
+    hop_send,
+    hop_recv,
+):
+    chips, pair, mine, spot, side = place_on_line()
+    section = lax.axis_index("section")
+    sections = lax.axis_size("section")
+    ticks, _, height, width = inputs.shape
+    local = gate.shape[0]
+    heads, head_size, latent = lookup.shape
+    context = keys.shape[1] - HALVES * height
+    chunk = width // RETURN_PIECES
+    step = height // PIECES
+    sibling = mine + 1 - 2 * side
+    at_end = (spot == 0) | (spot == chips - 1)
+    kind = rows_all.dtype
+
+    def wide(value):
+        return value.astype(jnp.float32)
+
+    def local_copy(source, target, sem):
+        return pltpu.make_async_copy(source, target, sem)
+
+    def input_copy(t, half):
+        source = opening_hbm.at[half] if t == 0 else incoming_hbm.at[t - 1, half]
+        return local_copy(source, inputs.at[t, half], input_sem.at[t, half])
+
+    def key_copy(t):
+        return local_copy(stored_hbm.at[t], keys.at[t, pl.ds(0, context)], key_sem.at[t])
+
+    attention_loads = [
+        local_copy(source, target, load_sem.at[index])
+        for index, (source, target) in enumerate(
+            (
+                (asking_hbm, asking),
+                (compress_hbm, compress),
+                (lookup_hbm, lookup),
+                (content_hbm, content),
+                (merging_hbm, merging),
+            )
+        )
+    ]
+    expert_loads = [
+        local_copy(source.at[e], target.at[e], gate_sem.at[index, e])
+        for e in range(local)
+        for index, (source, target) in enumerate(((gate_hbm, gate), (up_hbm, up), (down_hbm, down)))
+    ]
+
+    def reach(way):
+        return (spot < chips - 1) if way > 0 else (spot > 0)
+
+    def rows(t, block, half, piece):
+        first = pl.multiple_of(side * height + piece * step, step)
+        return rows_all.at[t, block, half, pl.ds(first, step)]
+
+    def line_copy(t, block, half, piece, way):
+        direction = 0 if way > 0 else 1
+        place = rows(t, block, half, piece)
+        return remote(
+            place,
+            place,
+            line_send.at[direction, block, half, piece],
+            line_recv.at[t, block, half, piece],
+            mine + way * pair,
+        )
+
+    def side_copy(t, block, half, piece):
+        place = rows(t, block, half, piece)
+        return remote(
+            place,
+            place,
+            side_send.at[block, half, piece],
+            side_recv.at[t, block, half, piece],
+            sibling,
+        )
+
+    def small_line_copy(block, way):
+        direction = 0 if way > 0 else 1
+        source = shares_ref if block is None else small_all.at[block, side]
+        where = spot if block is None else block
+        return remote(
+            source,
+            small_all.at[where, side],
+            small_line_send.at[direction, where],
+            small_line_recv.at[where],
+            mine + way * pair,
+        )
+
+    def small_side_copy(block):
+        source = shares_ref if block is None else small_all.at[block, side]
+        where = spot if block is None else block
+        return remote(
+            source,
+            small_all.at[where, side],
+            small_side_send.at[where],
+            small_side_recv.at[where],
+            sibling,
+        )
+
+    def give_copy(block, half, piece):
+        return remote(
+            part.at[block, half, 1 - side, piece],
+            side_in.at[block, half, piece],
+            give_send.at[block, half, piece],
+            give_recv.at[block, half, piece],
+            sibling,
+        )
+
+    def back_copy(block, half, piece, way, sender):
+        slot = jnp.where((block == sender + way) & (way < 0), chips, block)
+        return remote(
+            part.at[block, half, side, piece],
+            line_in.at[slot, half, piece],
+            back_send.at[block, half, piece],
+            back_recv.at[slot, half, piece],
+            mine + way * pair,
+        )
+
+    def combine(block, half, piece, way, from_line):
+        give_copy(block, half, piece).wait_recv()
+        value = wide(part[block, half, side, piece]) + wide(side_in[block, half, piece])
+        if from_line:
+            back_copy(block, half, piece, way, spot - way).wait_recv()
+            value = value + wide(line_in[block, half, piece])
+        part[block, half, side, piece] = value.astype(part.dtype)
+        back_copy(block, half, piece, way, spot).start()
+
+    def hop_copy(t, half, piece):
+        columns = pl.ds(piece * chunk, chunk)
+        return pltpu.make_async_remote_copy(
+            src_ref=results.at[t, half, :, columns],
+            dst_ref=inputs.at[t + 1, half, :, columns],
+            send_sem=hop_send.at[half, piece],
+            recv_sem=hop_recv.at[t + 1, half, piece],
+            device_id={"section": section + 1},
+            device_id_type=MESH,
+        )
+
+    def stream(way, unit, blocks):
+        first = unit < blocks
+        near = spot - way * (1 + unit)
+        back = unit - blocks
+        far = back if way > 0 else chips - 1 - back
+        return jnp.where(first, near, far), jnp.where(first, 0, 1)
+
+    def upstream(way):
+        return spot if way > 0 else chips - 1 - spot
+
+    def send_own(t, half, way):
+        for piece in range(PIECES):
+
+            @pl.when(reach(way))
+            def _():
+                line_copy(t, spot, half, piece, way).start()
+
+    def arrive(t, way, j):
+        blocks = upstream(way)
+        block, half = stream(way, lax.div(j, PIECES), blocks)
+        piece = lax.rem(j, PIECES)
+        line_copy(t, block, half, piece, way).wait_recv()
+
+        @pl.when(reach(way))
+        def _():
+            line_copy(t, block, half, piece, way).start()
+
+        side_copy(t, block, half, piece).start()
+
+        @pl.when(j == 2 * blocks * PIECES - 1)
+        def _():
+            send_own(t, 1, way)
+
+    def send_back(way, v):
+        ahead = upstream(-way)
+        block, half = stream(-way, lax.div(v, RETURN_PIECES), ahead)
+        combine(block, half, lax.rem(v, RETURN_PIECES), way, True)
+
+    def normed(values, gain):
+        mean = jnp.mean(values * values, axis=-1, keepdims=True)
+        return (values * lax.rsqrt(mean + epsilon) * gain).astype(kind)
+
+    def project(t):
+        values = inputs[t].reshape(HALVES * height, width)
+        rows_in = normed(wide(values), mixing_gain[...])
+        queries = jnp.dot(rows_in, asking[...], preferred_element_type=jnp.float32).astype(kind)
+        raw = jnp.dot(rows_in, compress[...], preferred_element_type=jnp.float32)
+        keys[t, context:] = normed(raw, latent_gain[...])
+        for head in range(heads):
+            part_of = queries[:, head * head_size : (head + 1) * head_size]
+            lat = jnp.dot(part_of, lookup[head], preferred_element_type=jnp.float32).astype(kind)
+            for half in range(HALVES):
+                q_lat[half, head * height : (head + 1) * height] = lat[
+                    half * height : (half + 1) * height
+                ]
+
+    def attend_half(t, half):
+        table = keys[t]
+        scores = lax.dot_general(q_lat[half], table, NT, preferred_element_type=jnp.float32)
+        scores = scores * head_size ** (-0.5)
+        position = lax.broadcasted_iota(jnp.int32, (height, table.shape[0]), 1)
+        query = lax.broadcasted_iota(jnp.int32, (height, table.shape[0]), 0) + half * height
+        limit = jnp.where(position < context, lengths[t], query + (context + 1))
+        visible = (position < limit)[None]
+        scores = scores.reshape((heads,) + position.shape)
+        scores = jnp.where(visible, scores, -jnp.inf).reshape(heads * height, -1)
+        expd = jnp.exp(scores - jnp.max(scores, axis=-1, keepdims=True))
+        weight = (expd * (1.0 / jnp.sum(expd, axis=-1, keepdims=True))).astype(kind)
+        o_lat = jnp.dot(weight, table, preferred_element_type=jnp.float32).astype(kind)
+        outs = []
+        for head in range(heads):
+            outs.append(
+                jnp.dot(
+                    o_lat[head * height : (head + 1) * height],
+                    content[head],
+                    preferred_element_type=jnp.float32,
+                ).astype(kind)
+            )
+        heads_out = jnp.concatenate(outs, axis=1)
+        total = wide(inputs[t, half]) + jnp.dot(
+            heads_out, merging[...], preferred_element_type=jnp.float32
+        )
+        residual[half] = total
+        first = pl.multiple_of(side * height, height)
+        rows_all[t, spot, half, pl.ds(first, height)] = normed(total, expert_gain[...])
+
+    def pass_small(far):
+        for way in (1, -1):
+            block = spot - way * far
+
+            @pl.when((block >= 0) if way > 0 else (block < chips))
+            def _():
+                small_line_copy(block, way).wait_recv()
+
+                @pl.when(reach(way))
+                def _():
+                    small_line_copy(block, way).start()
+
+                small_side_copy(block).start()
+
+    def poll(t, counts):
+        after = []
+        for way, count in zip((1, -1), counts):
+            total = 2 * upstream(way) * PIECES
+
+            @pl.when(count < total)
+            def _():
+                arrive(t, way, count)
+
+            after.append(jnp.minimum(count + 1, total))
+        return tuple(after)
+
+    def catch_up(t, way, count, goal):
+        def one(j, carry):
+            arrive(t, way, j)
+            return carry
+
+        lax.fori_loop(count, goal, one, 0)
+
+    units = 2 * chips
+    short = 2 * jnp.minimum(spot, chips - 1 - spot)
+    leftward = spot > chips - 1 - spot
+
+    def unit_of(k):
+        paired = k < 2 * short
+        unit = jnp.where(paired, lax.div(k, 2), k - short)
+        from_left = jnp.where(paired, lax.rem(k, 2) == 0, leftward)
+        left_block, left_half = stream(1, unit, upstream(1))
+        right_block, right_half = stream(-1, unit, upstream(-1))
+        own = k >= units - 2
+        block = jnp.where(own, spot, jnp.where(from_left, left_block, right_block))
+        half = jnp.where(own, k - units + 2, jnp.where(from_left, left_half, right_half))
+        need = jnp.where(own, 0, (unit + 1) * PIECES)
+        return block, half, jnp.where(from_left, need, 0), jnp.where(from_left, 0, need)
+
+    def visit(t, k, carry):
+        counts, sent = carry[:2], carry[2:]
+        block, half, _, _ = unit_of(k)
+        way = jnp.where(block > spot, 1, -1)
+        outward = at_end & (block != spot)
+        for piece in range(PIECES):
+            side_copy(t, block, half, piece).wait_recv()
+        values = rows_all[t, block, half]
+        for e in range(local):
+            line = mine * local + e + t * (small_all.shape[2] // ticks)
+            columns = []
+            for core in range(pair):
+                table = small_all[block, core]
+                here = lax.broadcasted_iota(jnp.int32, table.shape, 0) == line
+                row = jnp.sum(jnp.where(here, table, 0.0), axis=0, keepdims=True)
+                column = jnp.broadcast_to(row, (row.shape[1], row.shape[1])).T[:, :1]
+                columns.append(jnp.where(half == 0, column[:height], column[height:]))
+            share = jnp.concatenate(columns, axis=0)
+            gated = lax.dot_general(values, gate[e], NT, preferred_element_type=jnp.float32)
+            upped = lax.dot_general(values, up[e], NT, preferred_element_type=jnp.float32)
+            hidden[e] = (gated * jax.nn.sigmoid(gated) * upped * share).astype(kind)
+            counts = poll(t, counts)
+        for piece in range(RETURN_PIECES):
+            total = None
+            for e in range(local):
+                term = jnp.dot(
+                    hidden[e],
+                    down[e, :, piece * chunk : (piece + 1) * chunk],
+                    preferred_element_type=jnp.float32,
+                )
+                total = term if total is None else total + term
+            total = total.astype(part.dtype)
+            for core in range(pair):
+                part[block, half, core, piece] = total[core * height : (core + 1) * height]
+            give_copy(block, half, piece).start()
+            if piece > 0:
+
+                @pl.when(outward)
+                def _():
+                    combine(block, half, piece - 1, way, False)
+
+        @pl.when(outward)
+        def _():
+            combine(block, half, RETURN_PIECES - 1, way, False)
+
+        counts = poll(t, counts)
+        after = []
+        for direction, count in zip((1, -1), sent):
+            done = back_goal(direction, k)
+            goal = jnp.maximum(count, done)
+            return_up(direction, count, goal)
+            after.append(goal)
+        needs = unit_of(jnp.minimum(k + 1, units - 1))[2:]
+        ready = []
+        for direction, count, need in zip((1, -1), counts, needs):
+            goal = jnp.maximum(count, need)
+            catch_up(t, direction, count, goal)
+            ready.append(goal)
+        return (*ready, *after)
+
+    def back_total(way):
+        ahead = jnp.where(at_end, 0, upstream(-way))
+        return 2 * ahead * RETURN_PIECES
+
+    def back_goal(way, k):
+        due = lax.div(jnp.maximum(14 * k - 29 * upstream(way), 0), 5)
+        return jnp.minimum(due, back_total(way))
+
+    def return_up(way, count, goal):
+        def one(v, carry):
+            send_back(way, v)
+            return carry
+
+        lax.fori_loop(count, goal, one, 0)
+
+    def finish(t, half):
+        for piece in range(RETURN_PIECES):
+            columns = pl.ds(piece * chunk, chunk)
+            give_copy(spot, half, piece).wait_recv()
+            residual[half, :, columns] += wide(part[spot, half, side, piece]) + wide(
+                side_in[spot, half, piece]
+            )
+            for way in (1, -1):
+
+                @pl.when(reach(-way))
+                def _():
+                    back_copy(spot, half, piece, way, spot - way).wait_recv()
+                    slot = spot if way > 0 else chips
+                    residual[half, :, columns] += wide(line_in[slot, half, piece])
+
+            results[t, half, :, columns] = residual[half, :, columns].astype(kind)
+
+            @pl.when((section < sections - 1) & (t < ticks - 1))
+            def _():
+                hop_copy(t, half, piece).start()
+
+        local_copy(results.at[t, half], out_hbm.at[t, half], out_sem.at[t, half]).start()
+
+    barrier = pltpu.get_barrier_semaphore()
+
+    def hello(condition, device):
+        @pl.when(condition)
+        def _():
+            pl.semaphore_signal(barrier, inc=1, device_id=device, device_id_type=MESH)
+
+    for half in range(HALVES):
+        input_copy(0, half).start()
+    for load in attention_loads[:3]:
+        load.start()
+    key_copy(0).start()
+    for load in attention_loads[3:]:
+        load.start()
+    for load in expert_loads:
+        load.start()
+    keep_small = local_copy(shares_ref, small_all.at[spot, side], small_sem.at[0])
+    keep_small.start()
+    for t in range(1, ticks):
+        key_copy(t).start()
+
+        @pl.when(section == 0)
+        def _():
+            for half in range(HALVES):
+                input_copy(t, half).start()
+
+    line_neighbours = jnp.where(at_end, 1, 2)
+    section_neighbours = jnp.where((section == 0) | (section == sections - 1), 1, 2)
+    hello(spot > 0, {"expert": mine - pair})
+    hello(spot < chips - 1, {"expert": mine + pair})
+    hello(section > 0, {"section": section - 1})
+    hello(section < sections - 1, {"section": section + 1})
+    pl.semaphore_signal(barrier, inc=1, device_id={"expert": sibling}, device_id_type=MESH)
+    pl.semaphore_wait(barrier, 1 + line_neighbours + section_neighbours)
+
+    for way in (1, -1):
+
+        @pl.when(reach(way))
+        def _():
+            small_line_copy(None, way).start()
+
+    small_side_copy(None).start()
+    keep_small.wait()
+
+    def tick(t, carry):
+        for half in range(HALVES):
+
+            @pl.when((t == 0) | (section == 0))
+            def _():
+                local_copy(opening_hbm.at[half], inputs.at[t, half], input_sem.at[t, half]).wait()
+
+            @pl.when((t > 0) & (section > 0))
+            def _():
+                for piece in range(RETURN_PIECES):
+                    hop_copy(t - 1, half, piece).wait_recv()
+
+        @pl.when(t == 0)
+        def _():
+            for load in attention_loads[:3]:
+                load.wait()
+
+        project(t)
+        key_copy(t).wait()
+
+        @pl.when(t == 0)
+        def _():
+            for load in attention_loads[3:]:
+                load.wait()
+            if chips > 1:
+                pass_small(1)
+
+        for half in range(HALVES):
+            attend_half(t, half)
+            for piece in range(PIECES):
+                side_copy(t, spot, half, piece).start()
+            for way in (1, -1):
+                if half == 0:
+                    send_own(t, half, way)
+                else:
+
+                    @pl.when(upstream(way) == 0)
+                    def _():
+                        send_own(t, half, way)
+
+            if half == 0:
+
+                @pl.when(t == 0)
+                def _():
+                    for far in range(2, chips):
+                        pass_small(far)
+
+        @pl.when(t == 0)
+        def _():
+            for load in expert_loads:
+                load.wait()
+            small_side_copy(None).wait_recv()
+            for far in range(1, chips):
+                for way in (1, -1):
+                    block = spot - way * far
+
+                    @pl.when((block >= 0) if way > 0 else (block < chips))
+                    def _():
+                        small_side_copy(block).wait_recv()
+
+        start = []
+        for way in (1, -1):
+            goal = jnp.minimum(2 * upstream(way) * PIECES, PIECES)
+            catch_up(t, way, 0, goal)
+            start.append(goal)
+        none = jnp.int32(0)
+        state = lax.fori_loop(
+            0, units, lambda k, state: visit(t, k, state), (*start, none, none)
+        )
+        finish(t, 0)
+
+        def rest(v, carry):
+            for way, done in zip((1, -1), state[2:]):
+
+                @pl.when(done + v < back_total(way))
+                def _():
+                    send_back(way, done + v)
+
+            return carry
+
+        left_over = [back_total(way) - done for way, done in zip((1, -1), state[2:])]
+        lax.fori_loop(0, jnp.maximum(left_over[0], left_over[1]), rest, 0)
+        finish(t, 1)
+
+        def settle(block, inner):
+            for half in range(HALVES):
+                for piece in range(PIECES):
+                    for way in (1, -1):
+                        passes = (block <= spot) if way > 0 else (block >= spot)
+
+                        @pl.when(passes & reach(way))
+                        def _():
+                            line_copy(t, block, half, piece, way).wait_send()
+
+                    side_copy(t, block, half, piece).wait_send()
+                for piece in range(RETURN_PIECES):
+                    give_copy(block, half, piece).wait_send()
+
+                    @pl.when(block != spot)
+                    def _():
+                        back_copy(
+                            block, half, piece, jnp.where(block > spot, 1, -1), spot
+                        ).wait_send()
+
+            return inner
+
+        lax.fori_loop(0, chips, settle, 0)
+
+        @pl.when((section < sections - 1) & (t < ticks - 1))
+        def _():
+            for half in range(HALVES):
+                for piece in range(RETURN_PIECES):
+                    hop_copy(t, half, piece).wait_send()
+
+        return carry
+
+    lax.fori_loop(0, ticks, tick, 0)
+
+    def settle_small(block, carry):
+        for way in (1, -1):
+            passes = (block <= spot) if way > 0 else (block >= spot)
+
+            @pl.when(passes & reach(way))
+            def _():
+                small_line_copy(block, way).wait_send()
+
+        small_side_copy(block).wait_send()
+        return carry
+
+    lax.fori_loop(0, chips, settle_small, 0)
+    for t in range(ticks):
+        for half in range(HALVES):
+            local_copy(results.at[t, half], out_hbm.at[t, half], out_sem.at[t, half]).wait()
+
+
+def relay(
+    lengths,
+    shares,
+    mixing_gain,
+    latent_gain,
+    expert_gain,
+    opening,
+    incoming,
+    stored,
+    asking,
+    compress,
+    lookup,
+    content,
+    merging,
+    gate,
+    up,
+    down,
+):
+    count = lax.axis_size("expert")
+    pair = 2
+    chips = count // pair
+    ticks, context, latent = stored.shape
+    kind = opening.dtype
+    height = opening.shape[0] // HALVES
+    width = opening.shape[1]
+    local, inner = down.shape[:2]
+    heads = lookup.shape[0]
+    chunk = width // RETURN_PIECES
+    dma = pltpu.SemaphoreType.DMA
+    hbm = pl.BlockSpec(memory_space=pl.ANY)
+    vmem = pl.BlockSpec(memory_space=pltpu.VMEM)
+    smem = pl.BlockSpec(memory_space=pltpu.SMEM)
+    cut = (HALVES, height, width)
+    out = pl.pallas_call(
+        relay_kernel,
+        out_shape=jax.ShapeDtypeStruct((ticks,) + cut, kind),
+        in_specs=[smem] + [vmem] * 4 + [hbm] * 11,
+        out_specs=hbm,
+        scratch_shapes=[
+            *[pltpu.VMEM(w.shape, kind) for w in (asking, compress, lookup, content, merging)],
+            *[pltpu.VMEM((local, inner, width), kind) for _ in range(3)],
+            pltpu.VMEM((ticks, context + HALVES * height, latent), kind),
+            pltpu.VMEM((ticks,) + cut, kind),
+            pltpu.VMEM(cut, jnp.float32),
+            pltpu.VMEM((HALVES, heads * height, latent), kind),
+            pltpu.VMEM((ticks, chips, HALVES, pair * height, width), kind),
+            pltpu.VMEM((chips, pair) + shares.shape, shares.dtype),
+            pltpu.VMEM((local, pair * height, inner), kind),
+            pltpu.VMEM((chips, HALVES, pair, RETURN_PIECES, height, chunk), kind),
+            pltpu.VMEM((chips, HALVES, RETURN_PIECES, height, chunk), kind),
+            pltpu.VMEM((chips + 1, HALVES, RETURN_PIECES, height, chunk), kind),
+            pltpu.VMEM((ticks,) + cut, kind),
+            dma((ticks, HALVES)),
+            dma((5,)),
+            dma((3, local)),
+            dma((ticks,)),
+            dma((ticks, HALVES)),
+            dma((1,)),
+            dma((2, chips, HALVES, PIECES)),
+            dma((ticks, chips, HALVES, PIECES)),
+            dma((chips, HALVES, PIECES)),
+            dma((ticks, chips, HALVES, PIECES)),
+            dma((2, chips)),
+            dma((chips,)),
+            dma((chips,)),
+            dma((chips,)),
+            dma((chips, HALVES, RETURN_PIECES)),
+            dma((chips, HALVES, RETURN_PIECES)),
+            dma((chips, HALVES, RETURN_PIECES)),
+            dma((chips + 1, HALVES, RETURN_PIECES)),
+            dma((HALVES, RETURN_PIECES)),
+            dma((ticks, HALVES, RETURN_PIECES)),
+        ],
+        compiler_params=pltpu.CompilerParams(
+            collective_id=0, has_side_effects=True, vmem_limit_bytes=63 * 2**20
+        ),
+    )(
+        lengths,
+        shares,
+        mixing_gain,
+        latent_gain,
+        expert_gain,
+        opening.reshape(cut),
+        incoming.reshape((ticks - 1,) + cut),
+        stored,
+        asking,
+        compress,
+        lookup,
+        content,
+        merging,
+        gate,
+        up,
+        down,
+    )
+    return out.reshape(ticks, HALVES * height, width)
+
+
 def shifted(value, axis, steps):
     count = lax.axis_size(axis)
     initial, last = (max(0, -steps), min(count, count - steps))
@@ -435,6 +1139,27 @@
         axis=2,
     )
     shares_dense = jnp.swapaxes(shares_dense, 1, 2)
+    if lax.axis_size("tensor") == 1 and sources % 2 == 0 and section_count > 1 and tick_count > 1:
+        turns = jnp.arange(tick_count) - segment_ordinal + section_count - 1
+        routed_results = relay(
+            stored_counts[:, 0][turns],
+            shares_dense.reshape(tick_count * shares_dense.shape[1], piece_list),
+            mixing_scale_factor,
+            summary_scale_factor,
+            specialist_scale_factor,
+            opening_residual[0],
+            incoming_residual,
+            stored_summaries[:, 0, 0],
+            asking_projection[0],
+            compress_projection[0],
+            summary_lookup_factor[0],
+            summary_content_factor[0],
+            merging_projection[0],
+            jnp.swapaxes(specialist_switch_factor[0], 1, 2),
+            jnp.swapaxes(specialist_widen_factor[0], 1, 2),
+            specialist_contract_factor[0],
+        )
+        return routed_results[:, None]
     outputs = []
     present_carry = opening_residual[0]
     section_out = present_carry

time: 224 us -> 192 us (0.86)
  Pallas kernels: 139 us -> 184 us
  matrix products: 34.7 us -> 0 us
  other arithmetic: 24.1 us -> 0.63 us
  waiting for transfers between devices: 12.4 us -> 0 us
  local copies, waits for them, and re-layouts: 8.37 us -> 5.57 us
    pallas_call x2 -> x1, Pallas kernels: 139 us -> 184 us  [relay(): pl.pallas_call(relay_kernel, out_shape=jax.ShapeDtypeStruct((ticks,) + cu...]
    dot_general x10 -> x0, matrix products: 34.7 us -> none  [the longest x2 9.57 us: attend(): jnp.einsum('thl,kl->thk', q_lat, key_rows, preferred_element_type=jnp.flo...]
    sub x3 -> x0, other arithmetic: 14.6 us -> none  [the longest x2 14 us: attend(): expd = jnp.where(visible[:, None, :], jnp.exp(scores - row_max), 0.0)]
    ppermute x1 -> x0, waiting for transfers between devices: 12.4 us -> none  [shifted(): lax.ppermute(value, axis, [(source, source + steps) for source in range(i...]
    reduce_sum x2 -> x0, other arithmetic: 2.7 us -> none  [row_norm(): jnp.mean(values * values, axis=-1, keepdims=True) + epsilon]
    unnamed x28 -> x5, local copies, waits for them, and re-layouts: 6.71 us -> 4.34 us
  transfers between devices with their start and end apart: 1 -> 0, of which waited for: 1 -> 0; matrix products, arithmetic and copies ran while one was open for 0% -> 0% of each run, Pallas kernels for 0% -> 0%
where the time goes in v2:
time: 192 us; the launch traced here: 191 us
  Pallas kernels  184 us (96%)
  local copies, waits for them, and re-layouts  5.57 us (3%)
    pallas_call x1, Pallas kernels, relay(): pl.pallas_call(relay_kernel, out_shape=jax.ShapeDtypeStruct((ticks,) + cu...  184 us
    unnamed x5, local copies, waits for them, and re-layouts  4.34 us

profile of v2, /device:TPU:14, one launch (start us, length us, event | category | flops | bytes accessed | tf_op | source)
XLA Modules:
  0.0 190.6 jit_solution(10371406930485219976)
XLA Ops:
  0.0 0.0 copy-start
  0.0 0.6 copy-done
  0.7 1.2 gather_fusion
  1.9 0.7 copy.34
  2.6 0.7 copy.33
  3.3 0.6 select_reduce_fusion
  3.9 184.3 %shard_map.163 = bf16[2,2,64,2048]{3,2,1,0:T(8,128)(2,1)} custom-call(s32[2]{0:T(128)} %gather_fusion, f32[32,128]{1,0:T(8,128)} %bitcast.43, f32[1,2048]{1,0:T(1,128)} %mixing_gain.1, f32[1,512]{1,0:T(1,128)} %latent_gain.1, f32[1,2048]{1,0:T(1,128)} %expert_gain.1, bf16[2,64,2048]{2,1,0:T(8,128)(2,1)} %bitcast.41, bf16[1,2,64,2048]{3,2,1,0:T(8,128)(2,1)} %bitcast.42, ...), custom_call_target="tpu_custom_call" | custom-call | tf_op jit(solution)/shard_map/pallas_call | solution.py:1006
  188.3 2.3 %copy.36 = bf16[2,1,128,2048]{3,2,1,0:T(8,128)(2,1)} copy(bf16[2,1,128,2048]{3,2,1,0:T(8,128)(2,1)} %bitcast.34) | data formatting | bytes 2097152
  (4 shorter events, 0.0 us)
Async XLA Ops:
  0.0 0.7 copy-start

commit v3 on v2

--- a/solution.py
+++ b/solution.py
@@ -1,3 +1,5 @@
+import functools
+
 import jax
 import jax.numpy as jnp
 from jax import lax
@@ -366,68 +368,73 @@
 HALVES = 2
 
 
-def relay_kernel(
-    lengths,
-    shares_ref,
-    mixing_gain,
-    latent_gain,
-    expert_gain,
-    opening_hbm,
-    incoming_hbm,
-    stored_hbm,
-    asking_hbm,
-    compress_hbm,
-    lookup_hbm,
-    content_hbm,
-    merging_hbm,
-    gate_hbm,
-    up_hbm,
-    down_hbm,
-    out_hbm,
-    asking,
-    compress,
-    lookup,
-    content,
-    merging,
-    gate,
-    up,
-    down,
-    keys,
-    inputs,
-    residual,
-    q_lat,
-    rows_all,
-    small_all,
-    hidden,
-    part,
-    side_in,
-    line_in,
-    results,
-    input_sem,
-    load_sem,
-    gate_sem,
-    key_sem,
-    out_sem,
-    small_sem,
-    line_send,
-    line_recv,
-    side_send,
-    side_recv,
-    small_line_send,
-    small_line_recv,
-    small_side_send,
-    small_side_recv,
-    give_send,
-    give_recv,
-    back_send,
-    back_recv,
-    hop_send,
-    hop_recv,
-):
+def relay_kernel(ticks, *refs):
+    (
+        lengths,
+        picks_ref,
+        shares_ref,
+        mixing_gain,
+        latent_gain,
+        expert_gain,
+        opening_hbm,
+        incoming_hbm,
+        stored_hbm,
+        asking_hbm,
+        compress_hbm,
+        lookup_hbm,
+        content_hbm,
+        merging_hbm,
+        gate_hbm,
+        up_hbm,
+        down_hbm,
+    ) = refs[:17]
+    outs = refs[17 : 17 + ticks]
+    (
+        asking,
+        compress,
+        lookup,
+        content,
+        merging,
+        gate,
+        up,
+        down,
+        stage,
+        keys,
+        inputs,
+        residual,
+        q_lat,
+        rows_all,
+        small_all,
+        hidden,
+        part,
+        side_in,
+        line_in,
+        results,
+        input_sem,
+        load_sem,
+        down_sem,
+        stage_sem,
+        key_sem,
+        out_sem,
+        line_send,
+        line_recv,
+        side_send,
+        side_recv,
+        small_send,
+        small_recv,
+        give_send,
+        give_recv,
+        back_send,
+        back_recv,
+        hop_send,
+        hop_recv,
+    ) = refs[17 + ticks :]
     chips, pair, mine, spot, side = place_on_line()
     section = lax.axis_index("section")
     sections = lax.axis_size("section")
-    ticks, _, height, width = inputs.shape
+    _, _, height, width = inputs.shape
+    count = chips * pair
+    inner = down.shape[1]
     local = gate.shape[0]
     heads, head_size, latent = lookup.shape
     context = keys.shape[1] - HALVES * height
@@ -462,11 +469,46 @@
             )
         )
     ]
-    expert_loads = [
-        local_copy(source.at[e], target.at[e], gate_sem.at[index, e])
-        for e in range(local)
-        for index, (source, target) in enumerate(((gate_hbm, gate), (up_hbm, up), (down_hbm, down)))
-    ]
+    down_loads = [local_copy(down_hbm.at[e], down.at[e], down_sem.at[e]) for e in range(local)]
+    raw = [(source, target, e) for e in range(local) for source, target in ((gate_hbm, gate), (up_hbm, up))]
+    block_rows = stage.shape[1]
+    full = inner // block_rows
+    tail = inner - full * block_rows
+
+    def stage_copy(matrix, c, size):
+        source, _, e = raw[matrix]
+        first = pl.multiple_of(c * block_rows, block_rows)
+        return local_copy(
+            source.at[e, pl.ds(first, size)], stage.at[c, pl.ds(0, size)], stage_sem.at[c]
+        )
+
+    def stage_start(matrix):
+        for c in range(full):
+            stage_copy(matrix, c, block_rows).start()
+        if tail:
+            stage_copy(matrix, full, tail).start()
+
+    def turn_weights(counts):
+        for matrix in range(len(raw)):
+            _, target, e = raw[matrix]
+
+            def turn(c, carry):
+                stage_copy(matrix, c, block_rows).wait()
+                first = pl.multiple_of(c * block_rows, block_rows)
+                target[e, :, pl.ds(first, block_rows)] = stage[c].T
+                if matrix + 1 < len(raw):
+                    stage_copy(matrix + 1, c, block_rows).start()
+                return carry
+
+            lax.fori_loop(0, full, turn, 0)
+            if tail:
+                stage_copy(matrix, full, tail).wait()
+                target[e, :, full * block_rows :] = stage[full, :tail].T
+                if matrix + 1 < len(raw):
+                    stage_copy(matrix + 1, full, tail).start()
+
+            counts = poll(0, counts)
+        return counts
 
     def reach(way):
         return (spot < chips - 1) if way > 0 else (spot > 0)
@@ -496,27 +538,14 @@
             sibling,
         )
 
-    def small_line_copy(block, way):
-        direction = 0 if way > 0 else 1
-        source = shares_ref if block is None else small_all.at[block, side]
-        where = spot if block is None else block
+    def small_copy(distance):
+        place = small_all.at[spot, side]
         return remote(
-            source,
-            small_all.at[where, side],
-            small_line_send.at[direction, where],
-            small_line_recv.at[where],
-            mine + way * pair,
-        )
-
-    def small_side_copy(block):
-        source = shares_ref if block is None else small_all.at[block, side]
-        where = spot if block is None else block
-        return remote(
-            source,
-            small_all.at[where, side],
-            small_side_send.at[where],
-            small_side_recv.at[where],
-            sibling,
+            place,
+            place,
+            small_send.at[distance],
+            small_recv.at[distance],
+            lax.rem(mine + distance, count),
         )
 
     def give_copy(block, half, piece):
@@ -562,11 +591,11 @@
         first = unit < blocks
         near = spot - way * (1 + unit)
         back = unit - blocks
-        far = back if way > 0 else chips - 1 - back
+        far = jnp.where(way > 0, back, chips - 1 - back)
         return jnp.where(first, near, far), jnp.where(first, 0, 1)
 
     def upstream(way):
-        return spot if way > 0 else chips - 1 - spot
+        return jnp.where(way > 0, spot, chips - 1 - spot)
 
     def send_own(t, half, way):
         for piece in range(PIECES):
@@ -620,7 +649,7 @@
         scores = scores * head_size ** (-0.5)
         position = lax.broadcasted_iota(jnp.int32, (height, table.shape[0]), 1)
         query = lax.broadcasted_iota(jnp.int32, (height, table.shape[0]), 0) + half * height
-        limit = jnp.where(position < context, lengths[t], query + (context + 1))
+        limit = jnp.where(position < context, lengths[t - section + sections - 1], query + (context + 1))
         visible = (position < limit)[None]
         scores = scores.reshape((heads,) + position.shape)
         scores = jnp.where(visible, scores, -jnp.inf).reshape(heads * height, -1)
@@ -644,20 +673,6 @@
         first = pl.multiple_of(side * height, height)
         rows_all[t, spot, half, pl.ds(first, height)] = normed(total, expert_gain[...])
 
-    def pass_small(far):
-        for way in (1, -1):
-            block = spot - way * far
-
-            @pl.when((block >= 0) if way > 0 else (block < chips))
-            def _():
-                small_line_copy(block, way).wait_recv()
-
-                @pl.when(reach(way))
-                def _():
-                    small_line_copy(block, way).start()
-
-                small_side_copy(block).start()
-
     def poll(t, counts):
         after = []
         for way, count in zip((1, -1), counts):
@@ -680,24 +695,27 @@
     units = 2 * chips
     short = 2 * jnp.minimum(spot, chips - 1 - spot)
     leftward = spot > chips - 1 - spot
-
-    def unit_of(k):
-        paired = k < 2 * short
-        unit = jnp.where(paired, lax.div(k, 2), k - short)
-        from_left = jnp.where(paired, lax.rem(k, 2) == 0, leftward)
+    near_way = jnp.where(leftward, -1, 1)
+
+    def unit_of(k, lead):
+        own = (k < lead) | (k >= units - 2 + lead)
+        v = jnp.maximum(k - lead, 0)
+        paired = v < 2 * short
+        unit = jnp.where(paired, lax.div(v, 2), v - short)
+        from_left = jnp.where(paired, lax.rem(v, 2) == 0, leftward)
         left_block, left_half = stream(1, unit, upstream(1))
         right_block, right_half = stream(-1, unit, upstream(-1))
-        own = k >= units - 2
         block = jnp.where(own, spot, jnp.where(from_left, left_block, right_block))
-        half = jnp.where(own, k - units + 2, jnp.where(from_left, left_half, right_half))
+        half = jnp.where(own, jnp.where(k < units - 1, 0, 1), jnp.where(from_left, left_half, right_half))
         need = jnp.where(own, 0, (unit + 1) * PIECES)
         return block, half, jnp.where(from_left, need, 0), jnp.where(from_left, 0, need)
 
     def visit(t, k, carry):
         counts, sent = carry[:2], carry[2:]
-        block, half, _, _ = unit_of(k)
-        way = jnp.where(block > spot, 1, -1)
-        outward = at_end & (block != spot)
+        lead = jnp.where(t > 0, 1, 0)
+        block, half, _, _ = unit_of(k, lead)
+        done_block, done_half, _, _ = unit_of(jnp.maximum(k - 1, 0), lead)
+        outward = at_end & (done_block != spot) & (k > 0)
         for piece in range(PIECES):
             side_copy(t, block, half, piece).wait_recv()
         values = rows_all[t, block, half]
@@ -711,10 +729,18 @@
                 column = jnp.broadcast_to(row, (row.shape[1], row.shape[1])).T[:, :1]
                 columns.append(jnp.where(half == 0, column[:height], column[height:]))
             share = jnp.concatenate(columns, axis=0)
-            gated = lax.dot_general(values, gate[e], NT, preferred_element_type=jnp.float32)
-            upped = lax.dot_general(values, up[e], NT, preferred_element_type=jnp.float32)
+            gated = jnp.dot(values, gate[e], preferred_element_type=jnp.float32)
+            upped = jnp.dot(values, up[e], preferred_element_type=jnp.float32)
             hidden[e] = (gated * jax.nn.sigmoid(gated) * upped * share).astype(kind)
             counts = poll(t, counts)
+            if e == 0:
+
+                @pl.when(outward)
+                def _():
+                    way = jnp.where(done_block > spot, 1, -1)
+                    for piece in range(RETURN_PIECES):
+                        combine(done_block, done_half, piece, way, False)
+
         for piece in range(RETURN_PIECES):
             total = None
             for e in range(local):
@@ -728,24 +754,17 @@
             for core in range(pair):
                 part[block, half, core, piece] = total[core * height : (core + 1) * height]
             give_copy(block, half, piece).start()
-            if piece > 0:
-
-                @pl.when(outward)
-                def _():
-                    combine(block, half, piece - 1, way, False)
-
-        @pl.when(outward)
-        def _():
-            combine(block, half, RETURN_PIECES - 1, way, False)
+            if piece == RETURN_PIECES // 2 - 1:
+                counts = poll(t, counts)
 
         counts = poll(t, counts)
         after = []
-        for direction, count in zip((1, -1), sent):
-            done = back_goal(direction, k)
+        for direction, count in zip((near_way, -near_way), sent):
+            done = back_goal(direction, k + 1 - lead)
             goal = jnp.maximum(count, done)
             return_up(direction, count, goal)
             after.append(goal)
-        needs = unit_of(jnp.minimum(k + 1, units - 1))[2:]
+        needs = unit_of(jnp.minimum(k + 1, units - 1), lead)[2:]
         ready = []
         for direction, count, need in zip((1, -1), counts, needs):
             goal = jnp.maximum(count, need)
@@ -758,7 +777,7 @@
         return 2 * ahead * RETURN_PIECES
 
     def back_goal(way, k):
-        due = lax.div(jnp.maximum(14 * k - 29 * upstream(way), 0), 5)
+        due = lax.div(jnp.maximum(11 * k - 42 * upstream(way) + 12, 0), 4)
         return jnp.minimum(due, back_total(way))
 
     def return_up(way, count, goal):
@@ -789,7 +808,11 @@
             def _():
                 hop_copy(t, half, piece).start()
 
-        local_copy(results.at[t, half], out_hbm.at[t, half], out_sem.at[t, half]).start()
+        for i, out in enumerate(outs):
+
+            @pl.when(t == i)
+            def _():
+                local_copy(results.at[i, half], out.at[half], out_sem.at[i, half]).start()
 
     barrier = pltpu.get_barrier_semaphore()
 
@@ -803,37 +826,24 @@
     for load in attention_loads[:3]:
         load.start()
     key_copy(0).start()
-    for load in attention_loads[3:]:
-        load.start()
-    for load in expert_loads:
-        load.start()
-    keep_small = local_copy(shares_ref, small_all.at[spot, side], small_sem.at[0])
-    keep_small.start()
-    for t in range(1, ticks):
-        key_copy(t).start()
-
-        @pl.when(section == 0)
-        def _():
-            for half in range(HALVES):
-                input_copy(t, half).start()
-
-    line_neighbours = jnp.where(at_end, 1, 2)
+    experts_all = local * count
+    tokens = HALVES * height
+    for t in range(ticks):
+        table = jnp.zeros((experts_all, tokens), jnp.float32)
+        expert = lax.broadcasted_iota(jnp.int32, table.shape, 0)
+        for choice in range(picks_ref.shape[1]):
+            named = picks_ref[t, choice : choice + 1] == expert
+            table = table + jnp.where(named, shares_ref[t, choice : choice + 1], 0.0)
+        small_all[spot, side, t * experts_all : (t + 1) * experts_all] = table
+    for distance in range(1, count):
+        other = lax.rem(mine + distance, count)
+        pl.semaphore_signal(barrier, inc=1, device_id={"expert": other}, device_id_type=MESH)
     section_neighbours = jnp.where((section == 0) | (section == sections - 1), 1, 2)
-    hello(spot > 0, {"expert": mine - pair})
-    hello(spot < chips - 1, {"expert": mine + pair})
     hello(section > 0, {"section": section - 1})
     hello(section < sections - 1, {"section": section + 1})
-    pl.semaphore_signal(barrier, inc=1, device_id={"expert": sibling}, device_id_type=MESH)
-    pl.semaphore_wait(barrier, 1 + line_neighbours + section_neighbours)
-
-    for way in (1, -1):
-
-        @pl.when(reach(way))
-        def _():
-            small_line_copy(None, way).start()
-
-    small_side_copy(None).start()
-    keep_small.wait()
+    pl.semaphore_wait(barrier, count - 1 + section_neighbours)
+    for distance in range(1, count):
+        small_copy(distance).start()
 
     def tick(t, carry):
         for half in range(HALVES):
@@ -851,6 +861,8 @@
         def _():
             for load in attention_loads[:3]:
                 load.wait()
+            for load in attention_loads[3:]:
+                load.start()
 
         project(t)
         key_copy(t).wait()
@@ -859,8 +871,16 @@
         def _():
             for load in attention_loads[3:]:
                 load.wait()
-            if chips > 1:
-                pass_small(1)
+            stage_start(0)
+            for load in down_loads:
+                load.start()
+            for later in range(1, ticks):
+                key_copy(later).start()
+
+                @pl.when(section == 0)
+                def _():
+                    for half in range(HALVES):
+                        input_copy(later, half).start()
 
         for half in range(HALVES):
             attend_half(t, half)
@@ -875,39 +895,29 @@
                     def _():
                         send_own(t, half, way)
 
-            if half == 0:
-
-                @pl.when(t == 0)
-                def _():
-                    for far in range(2, chips):
-                        pass_small(far)
-
-        @pl.when(t == 0)
-        def _():
-            for load in expert_loads:
+        none = jnp.int32(0)
+
+        def first_tick():
+            counts = turn_weights((none, none))
+            for load in down_loads:
                 load.wait()
-            small_side_copy(None).wait_recv()
-            for far in range(1, chips):
-                for way in (1, -1):
-                    block = spot - way * far
-
-                    @pl.when((block >= 0) if way > 0 else (block < chips))
-                    def _():
-                        small_side_copy(block).wait_recv()
-
-        start = []
-        for way in (1, -1):
-            goal = jnp.minimum(2 * upstream(way) * PIECES, PIECES)
-            catch_up(t, way, 0, goal)
-            start.append(goal)
-        none = jnp.int32(0)
+            for distance in range(1, count):
+                small_copy(distance).wait_recv()
+            ready = []
+            for way, start, need in zip((1, -1), counts, unit_of(none, none)[2:]):
+                goal = jnp.maximum(start, need)
+                catch_up(0, way, start, goal)
+                ready.append(goal)
+            return tuple(ready)
+
+        counts = lax.cond(t == 0, first_tick, lambda: (none, none))
         state = lax.fori_loop(
-            0, units, lambda k, state: visit(t, k, state), (*start, none, none)
+            0, units, lambda k, state: visit(t, k, state), (*counts, none, none)
         )
         finish(t, 0)
 
         def rest(v, carry):
-            for way, done in zip((1, -1), state[2:]):
+            for way, done in zip((near_way, -near_way), state[2:]):
 
                 @pl.when(done + v < back_total(way))
                 def _():
@@ -915,7 +925,7 @@
 
             return carry
 
-        left_over = [back_total(way) - done for way, done in zip((1, -1), state[2:])]
+        left_over = [back_total(way) - done for way, done in zip((near_way, -near_way), state[2:])]
         lax.fori_loop(0, jnp.maximum(left_over[0], left_over[1]), rest, 0)
         finish(t, 1)
 
@@ -953,25 +963,16 @@
 
     lax.fori_loop(0, ticks, tick, 0)
 
-    def settle_small(block, carry):
-        for way in (1, -1):
-            passes = (block <= spot) if way > 0 else (block >= spot)
-
-            @pl.when(passes & reach(way))
-            def _():
-                small_line_copy(block, way).wait_send()
-
-        small_side_copy(block).wait_send()
-        return carry
-
-    lax.fori_loop(0, chips, settle_small, 0)
+    for distance in range(1, count):
+        small_copy(distance).wait_send()
     for t in range(ticks):
         for half in range(HALVES):
-            local_copy(results.at[t, half], out_hbm.at[t, half], out_sem.at[t, half]).wait()
+            local_copy(results.at[t, half], outs[t].at[half], out_sem.at[t, half]).wait()
 
 
 def relay(
     lengths,
+    picks,
     shares,
     mixing_gain,
     latent_gain,
@@ -1003,20 +1004,22 @@
     vmem = pl.BlockSpec(memory_space=pltpu.VMEM)
     smem = pl.BlockSpec(memory_space=pltpu.SMEM)
     cut = (HALVES, height, width)
-    out = pl.pallas_call(
-        relay_kernel,
-        out_shape=jax.ShapeDtypeStruct((ticks,) + cut, kind),
-        in_specs=[smem] + [vmem] * 4 + [hbm] * 11,
-        out_specs=hbm,
+    results = pl.pallas_call(
+        functools.partial(relay_kernel, ticks),
+        out_shape=[jax.ShapeDtypeStruct(cut, kind)] * ticks,
+        in_specs=[smem] + [vmem] * 5 + [hbm] * 11,
+        out_specs=[hbm] * ticks,
         scratch_shapes=[
             *[pltpu.VMEM(w.shape, kind) for w in (asking, compress, lookup, content, merging)],
-            *[pltpu.VMEM((local, inner, width), kind) for _ in range(3)],
+            *[pltpu.VMEM((local, width, inner), kind) for _ in range(2)],
+            pltpu.VMEM((local, inner, width), kind),
+            pltpu.VMEM((pl.cdiv(inner, 128), 128, width), kind),
             pltpu.VMEM((ticks, context + HALVES * height, latent), kind),
             pltpu.VMEM((ticks,) + cut, kind),
             pltpu.VMEM(cut, jnp.float32),
             pltpu.VMEM((HALVES, heads * height, latent), kind),
             pltpu.VMEM((ticks, chips, HALVES, pair * height, width), kind),
-            pltpu.VMEM((chips, pair) + shares.shape, shares.dtype),
+            pltpu.VMEM((chips, pair, ticks * local * count, HALVES * height), shares.dtype),
             pltpu.VMEM((local, pair * height, inner), kind),
             pltpu.VMEM((chips, HALVES, pair, RETURN_PIECES, height, chunk), kind),
             pltpu.VMEM((chips, HALVES, RETURN_PIECES, height, chunk), kind),
@@ -1024,18 +1027,16 @@
             pltpu.VMEM((ticks,) + cut, kind),
             dma((ticks, HALVES)),
             dma((5,)),
-            dma((3, local)),
+            dma((local,)),
+            dma((pl.cdiv(inner, 128),)),
             dma((ticks,)),
             dma((ticks, HALVES)),
-            dma((1,)),
             dma((2, chips, HALVES, PIECES)),
             dma((ticks, chips, HALVES, PIECES)),
             dma((chips, HALVES, PIECES)),
             dma((ticks, chips, HALVES, PIECES)),
-            dma((2, chips)),
-            dma((chips,)),
-            dma((chips,)),
-            dma((chips,)),
+            dma((count,)),
+            dma((count,)),
             dma((chips, HALVES, RETURN_PIECES)),
             dma((chips, HALVES, RETURN_PIECES)),
             dma((chips, HALVES, RETURN_PIECES)),
@@ -1048,6 +1049,7 @@
         ),
     )(
         lengths,
+        picks,
         shares,
         mixing_gain,
         latent_gain,
@@ -1064,7 +1066,7 @@
         up,
         down,
     )
-    return out.reshape(ticks, HALVES * height, width)
+    return jnp.stack([result.reshape(HALVES * height, width) for result in results])
 
 
 def shifted(value, axis, steps):
@@ -1129,21 +1131,11 @@
     top_count = picked_specialists.shape[3]
     expert_local = specialist_switch_factor.shape[1]
     score_scale = head_size ** (-0.5)
-    expert_ids = lax.broadcasted_iota(jnp.int32, (1, 1, 1, expert_local * sources), 3)
-    shares_dense = jnp.sum(
-        jnp.where(
-            picked_specialists[:, 0][..., None] == expert_ids,
-            chooser_mixing_share[:, 0][..., None],
-            0.0,
-        ),
-        axis=2,
-    )
-    shares_dense = jnp.swapaxes(shares_dense, 1, 2)
     if lax.axis_size("tensor") == 1 and sources % 2 == 0 and section_count > 1 and tick_count > 1:
-        turns = jnp.arange(tick_count) - segment_ordinal + section_count - 1
-        routed_results = relay(
-            stored_counts[:, 0][turns],
-            shares_dense.reshape(tick_count * shares_dense.shape[1], piece_list),
+        results = relay(
+            stored_counts[:, 0],
+            jnp.swapaxes(picked_specialists[:, 0], 1, 2),
+            jnp.swapaxes(chooser_mixing_share[:, 0], 1, 2),
             mixing_scale_factor,
             summary_scale_factor,
             specialist_scale_factor,
@@ -1159,7 +1151,17 @@
             jnp.swapaxes(specialist_widen_factor[0], 1, 2),
             specialist_contract_factor[0],
         )
-        return routed_results[:, None]
+        return results[:, None]
+    expert_ids = lax.broadcasted_iota(jnp.int32, (1, 1, 1, expert_local * sources), 3)
+    shares_dense = jnp.sum(
+        jnp.where(
+            picked_specialists[:, 0][..., None] == expert_ids,
+            chooser_mixing_share[:, 0][..., None],
+            0.0,
+        ),
+        axis=2,
+    )
+    shares_dense = jnp.swapaxes(shares_dense, 1, 2)
     outputs = []
     present_carry = opening_residual[0]
     section_out = present_carry

time: 192 us -> 136 us (0.71)
  Pallas kernels: 184 us -> 130 us
  local copies, waits for them, and re-layouts: 5.57 us -> 2.59 us
    pallas_call x1, Pallas kernels: 184 us -> 130 us  [relay(): pl.pallas_call(functools.partial(relay_kernel, ticks), out_shape=[jax.Sha...]
    unnamed x5 -> x2, local copies, waits for them, and re-layouts: 4.34 us -> 1.39 us
    broadcast_in_dim x0 -> x1, other arithmetic: none -> 2.27 us  [shards(): return results[:, None]]
where the time goes in v3:
time: 136 us; the launch traced here: 135 us
  Pallas kernels  130 us (96%)
  local copies, waits for them, and re-layouts  2.59 us (2%)
  other arithmetic  2.27 us (2%)
    pallas_call x1, Pallas kernels, relay(): pl.pallas_call(functools.partial(relay_kernel, ticks), out_shape=[jax.Sha...  130 us

profile of v3, /device:TPU:14, one launch (start us, length us, event | category | flops | bytes accessed | tf_op | source)
XLA Modules:
  0.0 134.7 jit_solution(1713226536951627856)
XLA Ops:
  0.0 0.7 copy.29
  0.7 0.6 copy.27
  1.3 0.7 copy.28
  2.0 0.6 copy.26
  2.6 129.9 %shard_map.163 = (bf16[2,64,2048]{2,1,0:T(8,128)(2,1)}, bf16[2,64,2048]{2,1,0:T(8,128)(2,1)}) custom-call(s32[3]{0:T(128)} %bitcast.49, s32[2,6,128]{2,1,0:T(8,128)} %bitcast.45, f32[2,6,128]{2,1,0:T(8,128)} %bitcast.46, f32[1,2048]{1,0:T(1,128)} %refs_3_.1, f32[1,512]{1,0:T(1,128)} %refs_4_.1, f32[1,2048]{1,0:T(1,128)} %refs_5_.1, ...), custom_call_target="tpu_custom_call" | custom-call | tf_op jit(solution)/shard_map/pallas_call | solution.py:1007
  132.5 2.3 %maximum_bitcast_fusion = bf16[2,1,128,2048]{3,2,1,0:T(8,128)(2,1)} fusion(bf16[1,128,2048]{2,1,0:T(8,128)(2,1)} %bitcast.44, bf16[1,128,2048]{2,1,0:T(8,128)(2,1)} %bitcast.43), kind=kLoop, calls=%fused_computation | loop fusion | flops 524288 | bytes 2097152 | tf_op jit(solution)/shard_map/broadcast_in_dim | solution.py:1154

commit v4 on v3

--- a/solution.py
+++ b/solution.py
@@ -388,7 +388,7 @@
         up_hbm,
         down_hbm,
     ) = refs[:17]
-    outs = refs[17 : 17 + ticks]
+    results = refs[17]
     (
         asking,
         compress,
@@ -409,13 +409,11 @@
         part,
         side_in,
         line_in,
-        results,
         input_sem,
         load_sem,
         down_sem,
         stage_sem,
         key_sem,
-        out_sem,
         line_send,
         line_recv,
         side_send,
@@ -428,7 +426,7 @@
         back_recv,
         hop_send,
         hop_recv,
-    ) = refs[17 + ticks :]
+    ) = refs[18:]
     chips, pair, mine, spot, side = place_on_line()
     section = lax.axis_index("section")
     sections = lax.axis_size("section")
@@ -523,7 +521,7 @@
         return remote(
             place,
             place,
-            line_send.at[direction, block, half, piece],
+            line_send.at[direction, block],
             line_recv.at[t, block, half, piece],
             mine + way * pair,
         )
@@ -533,10 +531,20 @@
         return remote(
             place,
             place,
-            side_send.at[block, half, piece],
-            side_recv.at[t, block, half, piece],
+            side_send.at[block],
+            side_recv.at[t, block, half],
             sibling,
         )
+
+    def whole_rows(t, block, half, other, send, recv):
+        place = rows_all.at[t, block, half, pl.ds(pl.multiple_of(side * height, height), height)]
+        return remote(place, place, send, recv, other)
+
+    def side_half(t, block, half):
+        return whole_rows(t, block, half, sibling, side_send.at[block], side_recv.at[t, block, half])
+
+    def all_sent(target, send):
+        remote(target, target, send, side_recv.at[0, 0, 0], sibling).wait_send()
 
     def small_copy(distance):
         place = small_all.at[spot, side]
@@ -552,7 +560,7 @@
         return remote(
             part.at[block, half, 1 - side, piece],
             side_in.at[block, half, piece],
-            give_send.at[block, half, piece],
+            give_send.at[block],
             give_recv.at[block, half, piece],
             sibling,
         )
@@ -562,7 +570,7 @@
         return remote(
             part.at[block, half, side, piece],
             line_in.at[slot, half, piece],
-            back_send.at[block, half, piece],
+            back_send.at[block],
             back_recv.at[slot, half, piece],
             mine + way * pair,
         )
@@ -581,8 +589,8 @@
         return pltpu.make_async_remote_copy(
             src_ref=results.at[t, half, :, columns],
             dst_ref=inputs.at[t + 1, half, :, columns],
-            send_sem=hop_send.at[half, piece],
-            recv_sem=hop_recv.at[t + 1, half, piece],
+            send_sem=hop_send.at[t],
+            recv_sem=hop_recv.at[t + 1, half],
             device_id={"section": section + 1},
             device_id_type=MESH,
         )
@@ -629,22 +637,26 @@
         mean = jnp.mean(values * values, axis=-1, keepdims=True)
         return (values * lax.rsqrt(mean + epsilon) * gain).astype(kind)
 
-    def project(t):
-        values = inputs[t].reshape(HALVES * height, width)
+    def first_only(t, act):
+        @pl.when(t == 0)
+        def _():
+            act()
+
+    def project(t, halves):
+        values = jnp.concatenate([inputs[t, half] for half in halves], axis=0)
         rows_in = normed(wide(values), mixing_gain[...])
         queries = jnp.dot(rows_in, asking[...], preferred_element_type=jnp.float32).astype(kind)
         raw = jnp.dot(rows_in, compress[...], preferred_element_type=jnp.float32)
-        keys[t, context:] = normed(raw, latent_gain[...])
+        first = context + halves[0] * height
+        keys[t, first : first + len(halves) * height] = normed(raw, latent_gain[...])
         for head in range(heads):
             part_of = queries[:, head * head_size : (head + 1) * head_size]
             lat = jnp.dot(part_of, lookup[head], preferred_element_type=jnp.float32).astype(kind)
-            for half in range(HALVES):
-                q_lat[half, head * height : (head + 1) * height] = lat[
-                    half * height : (half + 1) * height
-                ]
+            for i, half in enumerate(halves):
+                q_lat[half, head * height : (head + 1) * height] = lat[i * height : (i + 1) * height]
 
     def attend_half(t, half):
-        table = keys[t]
+        table = keys[t, : context + (half + 1) * height]
         scores = lax.dot_general(q_lat[half], table, NT, preferred_element_type=jnp.float32)
         scores = scores * head_size ** (-0.5)
         position = lax.broadcasted_iota(jnp.int32, (height, table.shape[0]), 1)
@@ -716,8 +728,18 @@
         block, half, _, _ = unit_of(k, lead)
         done_block, done_half, _, _ = unit_of(jnp.maximum(k - 1, 0), lead)
         outward = at_end & (done_block != spot) & (k > 0)
-        for piece in range(PIECES):
-            side_copy(t, block, half, piece).wait_recv()
+        side_half(t, block, half).wait_recv()
+
+        @pl.when(outward)
+        def _():
+            way = jnp.where(done_block > spot, 1, -1)
+            for piece in range(RETURN_PIECES):
+                combine(done_block, done_half, piece, way, False)
+
+        @pl.when((k == units - 1) & (lead == 0))
+        def _():
+            finish(t, 0)
+
         values = rows_all[t, block, half]
         for e in range(local):
             line = mine * local + e + t * (small_all.shape[2] // ticks)
@@ -734,13 +756,7 @@
             hidden[e] = (gated * jax.nn.sigmoid(gated) * upped * share).astype(kind)
             counts = poll(t, counts)
             if e == 0:
-
-                @pl.when(outward)
-                def _():
-                    way = jnp.where(done_block > spot, 1, -1)
-                    for piece in range(RETURN_PIECES):
-                        combine(done_block, done_half, piece, way, False)
-
+                sent = send_due(sent, 2 * k - 1, k - lead)
         for piece in range(RETURN_PIECES):
             total = None
             for e in range(local):
@@ -758,12 +774,7 @@
                 counts = poll(t, counts)
 
         counts = poll(t, counts)
-        after = []
-        for direction, count in zip((near_way, -near_way), sent):
-            done = back_goal(direction, k + 1 - lead)
-            goal = jnp.maximum(count, done)
-            return_up(direction, count, goal)
-            after.append(goal)
+        after = send_due(sent, 2 * k, k - lead + 1)
         needs = unit_of(jnp.minimum(k + 1, units - 1), lead)[2:]
         ready = []
         for direction, count, need in zip((1, -1), counts, needs):
@@ -776,9 +787,22 @@
         ahead = jnp.where(at_end, 0, upstream(-way))
         return 2 * ahead * RETURN_PIECES
 
-    def back_goal(way, k):
-        due = lax.div(jnp.maximum(11 * k - 42 * upstream(way) + 12, 0), 4)
-        return jnp.minimum(due, back_total(way))
+    def back_goal(way, moment, seen):
+        beyond = upstream(way) - 1
+        due = lax.div(jnp.maximum(11 * moment - 32 - beyond * (moment + 50), 0), 8)
+        seen = jnp.clip(seen, 0, units - 2)
+        longer = jnp.where(leftward, way < 0, way > 0)
+        paired = lax.div(seen + jnp.where(way < 0, 1, 0), 2)
+        held = jnp.where(seen <= 2 * short, paired, jnp.where(longer, seen - short, short))
+        return jnp.minimum(jnp.minimum(due, held * RETURN_PIECES), back_total(way))
+
+    def send_due(sent, moment, seen):
+        after = []
+        for direction, count in zip((near_way, -near_way), sent):
+            goal = jnp.maximum(count, back_goal(direction, moment, seen))
+            return_up(direction, count, goal)
+            after.append(goal)
+        return tuple(after)
 
     def return_up(way, count, goal):
         def one(v, carry):
@@ -807,12 +831,6 @@
             @pl.when((section < sections - 1) & (t < ticks - 1))
             def _():
                 hop_copy(t, half, piece).start()
-
-        for i, out in enumerate(outs):
-
-            @pl.when(t == i)
-            def _():
-                local_copy(results.at[i, half], out.at[half], out_sem.at[i, half]).start()
 
     barrier = pltpu.get_barrier_semaphore()
 
@@ -832,8 +850,8 @@
         table = jnp.zeros((experts_all, tokens), jnp.float32)
         expert = lax.broadcasted_iota(jnp.int32, table.shape, 0)
         for choice in range(picks_ref.shape[1]):
-            named = picks_ref[t, choice : choice + 1] == expert
-            table = table + jnp.where(named, shares_ref[t, choice : choice + 1], 0.0)
+            named = picks_ref[t, choice] == expert
+            table = table + jnp.where(named, shares_ref[t, choice], 0.0)
         small_all[spot, side, t * experts_all : (t + 1) * experts_all] = table
     for distance in range(1, count):
         other = lax.rem(mine + distance, count)
@@ -846,29 +864,16 @@
         small_copy(distance).start()
 
     def tick(t, carry):
-        for half in range(HALVES):
-
-            @pl.when((t == 0) | (section == 0))
-            def _():
-                local_copy(opening_hbm.at[half], inputs.at[t, half], input_sem.at[t, half]).wait()
-
-            @pl.when((t > 0) & (section > 0))
-            def _():
-                for piece in range(RETURN_PIECES):
-                    hop_copy(t - 1, half, piece).wait_recv()
-
         @pl.when(t == 0)
         def _():
+            for half in range(HALVES):
+                input_copy(0, half).wait()
             for load in attention_loads[:3]:
                 load.wait()
             for load in attention_loads[3:]:
                 load.start()
-
-        project(t)
-        key_copy(t).wait()
-
-        @pl.when(t == 0)
-        def _():
+            project(0, tuple(range(HALVES)))
+            key_copy(0).wait()
             for load in attention_loads[3:]:
                 load.wait()
             stage_start(0)
@@ -883,6 +888,22 @@
                         input_copy(later, half).start()
 
         for half in range(HALVES):
+
+            @pl.when(t > 0)
+            def _():
+                @pl.when(section == 0)
+                def _():
+                    local_copy(opening_hbm.at[half], inputs.at[t, half], input_sem.at[t, half]).wait()
+
+                @pl.when(section > 0)
+                def _():
+                    place = inputs.at[t, half]
+                    remote(place, place, hop_send.at[0], hop_recv.at[t, half], sibling).wait_recv()
+
+                project(t, (half,))
+                if half == 0:
+                    key_copy(t).wait()
+
             attend_half(t, half)
             for piece in range(PIECES):
                 side_copy(t, spot, half, piece).start()
@@ -914,7 +935,9 @@
         state = lax.fori_loop(
             0, units, lambda k, state: visit(t, k, state), (*counts, none, none)
         )
-        finish(t, 0)
+        @pl.when(t > 0)
+        def _():
+            finish(t, 0)
 
         def rest(v, carry):
             for way, done in zip((near_way, -near_way), state[2:]):
@@ -930,44 +953,36 @@
         finish(t, 1)
 
         def settle(block, inner):
-            for half in range(HALVES):
-                for piece in range(PIECES):
-                    for way in (1, -1):
-                        passes = (block <= spot) if way > 0 else (block >= spot)
-
-                        @pl.when(passes & reach(way))
-                        def _():
-                            line_copy(t, block, half, piece, way).wait_send()
-
-                    side_copy(t, block, half, piece).wait_send()
-                for piece in range(RETURN_PIECES):
-                    give_copy(block, half, piece).wait_send()
-
-                    @pl.when(block != spot)
-                    def _():
-                        back_copy(
-                            block, half, piece, jnp.where(block > spot, 1, -1), spot
-                        ).wait_send()
+            owned = pl.ds(pl.multiple_of(side * height, height), height)
+            for way in (1, -1):
+                passes = (block <= spot) if way > 0 else (block >= spot)
+
+                @pl.when(passes & reach(way))
+                def _():
+                    direction = 0 if way > 0 else 1
+                    all_sent(rows_all.at[t, block, :, owned], line_send.at[direction, block])
+
+            all_sent(rows_all.at[t, block, :, owned], side_send.at[block])
+            all_sent(part.at[block, :, 1 - side], give_send.at[block])
+
+            @pl.when(block != spot)
+            def _():
+                all_sent(part.at[block, :, side], back_send.at[block])
 
             return inner
 
         lax.fori_loop(0, chips, settle, 0)
-
-        @pl.when((section < sections - 1) & (t < ticks - 1))
-        def _():
-            for half in range(HALVES):
-                for piece in range(RETURN_PIECES):
-                    hop_copy(t, half, piece).wait_send()
-
         return carry
 
     lax.fori_loop(0, ticks, tick, 0)
 
     for distance in range(1, count):
         small_copy(distance).wait_send()
-    for t in range(ticks):
-        for half in range(HALVES):
-            local_copy(results.at[t, half], outs[t].at[half], out_sem.at[t, half]).wait()
+    for t in range(ticks - 1):
+
+        @pl.when(section < sections - 1)
+        def _():
+            all_sent(results.at[t], hop_send.at[t])
 
 
 def relay(
@@ -1004,11 +1019,11 @@
     vmem = pl.BlockSpec(memory_space=pltpu.VMEM)
     smem = pl.BlockSpec(memory_space=pltpu.SMEM)
     cut = (HALVES, height, width)
-    results = pl.pallas_call(
+    return pl.pallas_call(
         functools.partial(relay_kernel, ticks),
-        out_shape=[jax.ShapeDtypeStruct(cut, kind)] * ticks,
+        out_shape=jax.ShapeDtypeStruct((ticks,) + cut, kind),
         in_specs=[smem] + [vmem] * 5 + [hbm] * 11,
-        out_specs=[hbm] * ticks,
+        out_specs=vmem,
         scratch_shapes=[
             *[pltpu.VMEM(w.shape, kind) for w in (asking, compress, lookup, content, merging)],
             *[pltpu.VMEM((local, width, inner), kind) for _ in range(2)],
@@ -1024,28 +1039,26 @@
             pltpu.VMEM((chips, HALVES, pair, RETURN_PIECES, height, chunk), kind),
             pltpu.VMEM((chips, HALVES, RETURN_PIECES, height, chunk), kind),
             pltpu.VMEM((chips + 1, HALVES, RETURN_PIECES, height, chunk), kind),
-            pltpu.VMEM((ticks,) + cut, kind),
             dma((ticks, HALVES)),
             dma((5,)),
             dma((local,)),
             dma((pl.cdiv(inner, 128),)),
             dma((ticks,)),
-            dma((ticks, HALVES)),
-            dma((2, chips, HALVES, PIECES)),
+            dma((2, chips)),
             dma((ticks, chips, HALVES, PIECES)),
-            dma((chips, HALVES, PIECES)),
-            dma((ticks, chips, HALVES, PIECES)),
+            dma((chips,)),
+            dma((ticks, chips, HALVES)),
             dma((count,)),
             dma((count,)),
+            dma((chips,)),
             dma((chips, HALVES, RETURN_PIECES)),
-            dma((chips, HALVES, RETURN_PIECES)),
-            dma((chips, HALVES, RETURN_PIECES)),
+            dma((chips,)),
             dma((chips + 1, HALVES, RETURN_PIECES)),
-            dma((HALVES, RETURN_PIECES)),
-            dma((ticks, HALVES, RETURN_PIECES)),
+            dma((ticks,)),
+            dma((ticks, HALVES)),
         ],
         compiler_params=pltpu.CompilerParams(
-            collective_id=0, has_side_effects=True, vmem_limit_bytes=63 * 2**20
+            collective_id=0, has_side_effects=True, vmem_limit_bytes=58 * 2**20
         ),
     )(
         lengths,
@@ -1065,8 +1078,7 @@
         gate,
         up,
         down,
-    )
-    return jnp.stack([result.reshape(HALVES * height, width) for result in results])
+    ).reshape(ticks, HALVES * height, width)
 
 
 def shifted(value, axis, steps):
@@ -1134,8 +1146,8 @@
     if lax.axis_size("tensor") == 1 and sources % 2 == 0 and section_count > 1 and tick_count > 1:
         results = relay(
             stored_counts[:, 0],
-            jnp.swapaxes(picked_specialists[:, 0], 1, 2),
-            jnp.swapaxes(chooser_mixing_share[:, 0], 1, 2),
+            jnp.transpose(picked_specialists, (0, 3, 1, 2)),
+            jnp.transpose(chooser_mixing_share, (0, 3, 1, 2)),
             mixing_scale_factor,
             summary_scale_factor,
             specialist_scale_factor,

time: 136 us -> 125 us (0.919)
  Pallas kernels: 130 us -> 122 us
  other arithmetic: 2.27 us -> 0 us
    pallas_call x1, Pallas kernels: 130 us -> 122 us  [relay(): pl.pallas_call(functools.partial(relay_kernel, ticks), out_shape=jax.Shap...]
    broadcast_in_dim x1 -> x0, other arithmetic: 2.27 us -> none  [shards(): return results[:, None]]
where the time goes in v4:
time: 125 us; the launch traced here: 124 us
  Pallas kernels  122 us (98%)
  local copies, waits for them, and re-layouts  2.3 us (2%)
    pallas_call x1, Pallas kernels, relay(): pl.pallas_call(functools.partial(relay_kernel, ticks), out_shape=jax.Shap...  122 us

profile of v4, /device:TPU:14, one launch (start us, length us, event | category | flops | bytes accessed | tf_op | source)
XLA Modules:
  0.0 124.4 jit_solution(3091892165479727926)
XLA Ops:
  0.0 122.1 %shard_map.163 = bf16[2,2,64,2048]{3,2,1,0:T(8,128)(2,1)} custom-call(s32[3]{0:T(128)} %bitcast.35, s32[2,6,1,128]{3,2,1,0:T(1,128)} %bitcast.33, f32[2,6,1,128]{3,2,1,0:T(1,128)} %bitcast.34, f32[1,2048]{1,0:T(1,128)} %refs_3_.1, f32[1,512]{1,0:T(1,128)} %refs_4_.1, f32[1,2048]{1,0:T(1,128)} %refs_5_.1, bf16[2,64,2048]{2,1,0:T(8,128)(2,1)} %bitcast.31, ...), custom_call_target="tpu_custom_call" | custom-call | tf_op jit(solution)/shard_map/pallas_call | solution.py:1022
  122.1 2.3 %copy.20 = bf16[2,1,128,2048]{3,2,1,0:T(8,128)(2,1)} copy(bf16[2,1,128,2048]{3,2,1,0:T(8,128)(2,1)} %bitcast.26) | data formatting | bytes 2097152

commit v5 on v4

--- a/solution.py
+++ b/solution.py
@@ -728,12 +728,13 @@
         block, half, _, _ = unit_of(k, lead)
         done_block, done_half, _, _ = unit_of(jnp.maximum(k - 1, 0), lead)
         outward = at_end & (done_block != spot) & (k > 0)
+        slack = 28 + 26 * lead
         side_half(t, block, half).wait_recv()
 
         @pl.when(outward)
         def _():
             way = jnp.where(done_block > spot, 1, -1)
-            for piece in range(RETURN_PIECES):
+            for piece in range(RETURN_PIECES // 2, RETURN_PIECES):
                 combine(done_block, done_half, piece, way, False)
 
         @pl.when((k == units - 1) & (lead == 0))
@@ -756,7 +757,7 @@
             hidden[e] = (gated * jax.nn.sigmoid(gated) * upped * share).astype(kind)
             counts = poll(t, counts)
             if e == 0:
-                sent = send_due(sent, 2 * k - 1, k - lead)
+                sent = send_due(sent, 2 * k - 1, k - lead, slack)
         for piece in range(RETURN_PIECES):
             total = None
             for e in range(local):
@@ -774,7 +775,14 @@
                 counts = poll(t, counts)
 
         counts = poll(t, counts)
-        after = send_due(sent, 2 * k, k - lead + 1)
+
+        @pl.when(at_end & (block != spot))
+        def _():
+            way = jnp.where(block > spot, 1, -1)
+            for piece in range(RETURN_PIECES // 2):
+                combine(block, half, piece, way, False)
+
+        after = send_due(sent, 2 * k, k - lead + 1, slack)
         needs = unit_of(jnp.minimum(k + 1, units - 1), lead)[2:]
         ready = []
         for direction, count, need in zip((1, -1), counts, needs):
@@ -787,19 +795,19 @@
         ahead = jnp.where(at_end, 0, upstream(-way))
         return 2 * ahead * RETURN_PIECES
 
-    def back_goal(way, moment, seen):
+    def back_goal(way, moment, seen, slack):
         beyond = upstream(way) - 1
-        due = lax.div(jnp.maximum(11 * moment - 32 - beyond * (moment + 50), 0), 8)
+        due = lax.div(jnp.maximum(11 * moment - slack - beyond * (moment + 46), 0), 8)
         seen = jnp.clip(seen, 0, units - 2)
         longer = jnp.where(leftward, way < 0, way > 0)
         paired = lax.div(seen + jnp.where(way < 0, 1, 0), 2)
         held = jnp.where(seen <= 2 * short, paired, jnp.where(longer, seen - short, short))
         return jnp.minimum(jnp.minimum(due, held * RETURN_PIECES), back_total(way))
 
-    def send_due(sent, moment, seen):
+    def send_due(sent, moment, seen, slack):
         after = []
         for direction, count in zip((near_way, -near_way), sent):
-            goal = jnp.maximum(count, back_goal(direction, moment, seen))
+            goal = jnp.maximum(count, back_goal(direction, moment, seen, slack))
             return_up(direction, count, goal)
             after.append(goal)
         return tuple(after)

time: 125 us -> 122 us (0.976)
  Pallas kernels: 122 us -> 119 us
    pallas_call x1, Pallas kernels: 122 us -> 119 us  [relay(): pl.pallas_call(functools.partial(relay_kernel, ticks), out_shape=jax.Shap...]
where the time goes in v5:
time: 122 us; the launch traced here: 121 us
  Pallas kernels  119 us (98%)
  local copies, waits for them, and re-layouts  2.3 us (2%)
    pallas_call x1, Pallas kernels, relay(): pl.pallas_call(functools.partial(relay_kernel, ticks), out_shape=jax.Shap...  119 us

profile of v5, /device:TPU:14, one launch (start us, length us, event | category | flops | bytes accessed | tf_op | source)
XLA Modules:
  0.0 120.9 jit_solution(12421008256427685283)
XLA Ops:
  0.0 118.6 %shard_map.163 = bf16[2,2,64,2048]{3,2,1,0:T(8,128)(2,1)} custom-call(s32[3]{0:T(128)} %bitcast.35, s32[2,6,1,128]{3,2,1,0:T(1,128)} %bitcast.33, f32[2,6,1,128]{3,2,1,0:T(1,128)} %bitcast.34, f32[1,2048]{1,0:T(1,128)} %refs_3_.1, f32[1,512]{1,0:T(1,128)} %refs_4_.1, f32[1,2048]{1,0:T(1,128)} %refs_5_.1, bf16[2,64,2048]{2,1,0:T(8,128)(2,1)} %bitcast.31, ...), custom_call_target="tpu_custom_call" | custom-call | tf_op jit(solution)/shard_map/pallas_call | solution.py:1030
  118.6 2.3 %copy.20 = bf16[2,1,128,2048]{3,2,1,0:T(8,128)(2,1)} copy(bf16[2,1,128,2048]{3,2,1,0:T(8,128)(2,1)} %bitcast.26) | data formatting | bytes 2097152
